TPU v7x, 128 devices: a whole 4x4x4 slice. The times are simulated.
128 devices in a mesh: dp: 32 (over z, y, x_hi), mp: 4 (over x_lo, core).
Axes of the slice: x: 4 (x_hi: 2, x_lo: 2; x = x_hi * 2 + x_lo), y: 4, z: 4, core: 2. Of those that a mesh axis runs over, the one named last changes fastest.
Arguments:
- tokens: bfloat16 [2, 4096, 2048], P(None, 'dp'), may hold values from -6 to 6
- segment_ids: int32 [2, 4096], replicated, may hold values from 0 to 1, never falling along the last dimension, each value on 1 to 3584 neighbouring positions
- skip_mask: int32 [2, 2], replicated, may hold values 0 or 1
- norm1_gain: bfloat16 [2048], P('dp'), may hold values from 0.25 to 1.75
- w_query: bfloat16 [2048, 2048], P('dp', 'mp'), may hold values from -0.125 to 0.125
- w_key: bfloat16 [2048, 512], P('dp', 'mp'), may hold values from -0.125 to 0.125
- w_value: bfloat16 [2048, 512], P('dp', 'mp'), may hold values from -0.125 to 0.125
- w_out: bfloat16 [2048, 2048], P('mp', 'dp'), may hold values from -1 to 1
- norm2_gain: bfloat16 [2048], P('dp'), may hold values from 0.25 to 1.75
- w_gate: bfloat16 [2048, 5632], P('dp', 'mp'), may hold values from -0.125 to 0.125
- w_up: bfloat16 [2048, 5632], P('dp', 'mp'), may hold values from -0.125 to 0.125
- w_down: bfloat16 [5632, 2048], P('mp', 'dp'), may hold values from -0.078125 to 0.078125
- cotangent: bfloat16 [2, 4096, 2048], P(None, 'dp'), may hold values from -6 to 6
Outputs:
- result: bfloat16 [2, 4096, 2048], P(None, 'dp')
- d_tokens: bfloat16 [2, 4096, 2048], P(None, 'dp')
- d_norm1_gain: float32 [2048], P('dp')
- d_w_query: float32 [2048, 2048], P('dp', 'mp')
- d_w_key: float32 [2048, 512], P('dp', 'mp')
- d_w_value: float32 [2048, 512], P('dp', 'mp')
- d_w_out: float32 [2048, 2048], P('mp', 'dp')
- d_norm2_gain: float32 [2048], P('dp')
- d_w_gate: float32 [2048, 5632], P('dp', 'mp')
- d_w_up: float32 [2048, 5632], P('dp', 'mp')
- d_w_down: float32 [5632, 2048], P('mp', 'dp')
Inputs may be any that keep to these rules, and one draw needn't show every extreme that they name: `segment_ids`: document numbers never fall along a micro-batch; 2 documents of 1 to 3584 tokens each.
All inputs are finite; a program needn't handle non-finite values.
Results may differ from a plain program's by a relative error of at most 0.03.
Values may be sent and summed in bfloat16 or wider, within the bound.
No kernel may reach another device: no remote copies, remote signals or barrier semaphores. Data moves between devices by JAX's collectives and lax.ppermute only.
A program may use at most 192 MiB of HBM per device.

v0:
```python
import math

import jax
import jax.numpy as jnp
from jax import lax
from jax.sharding import Mesh
from jax.sharding import PartitionSpec as P

HD = 128
BLOCK = 256
DP = ("dp_0", "dp_1", "dp_2")


EPSILON = 1e-05
NEGATIVE = -1e30


def in_one_piece(arrays, axis, dim, along):
    columns = [a.reshape(*a.shape[:along], -1) for a in arrays]
    both = jnp.concatenate(columns, axis=along)
    filled, at, done = (lax.all_gather(both, axis, axis=dim, tiled=True), 0, [])
    for a, column in zip(arrays, columns):
        share = filled[..., at : at + column.shape[along]]
        done.append(share.reshape(*share.shape[:along], *a.shape[along:]))
        at += column.shape[along]
    return tuple(done)


def gather_turned(arrays, axis, dims):
    turned = [jnp.moveaxis(a, dim, 0) for a, dim in zip(arrays, dims)]
    both = jnp.concatenate([t.reshape(len(t), -1) for t in turned], axis=1)
    filled, at, done = (lax.all_gather(both, axis, axis=0, tiled=True), 0, [])
    for t, dim in zip(turned, dims):
        share = filled[:, at : at + t[0].size].reshape(-1, *t.shape[1:])
        done.append(jnp.moveaxis(share, 0, dim))
        at += t[0].size
    return tuple(done)


def for_sending(value):
    return jax.tree.map(lambda a: a.astype(jnp.bfloat16) if a.dtype == jnp.float32 else a, value)


def summed_rows(value, axes, dim):
    for axis in axes:
        value = lax.psum_scatter(value, axis, scatter_dimension=dim, tiled=True)
    return value


def side_by_side(arrays, axis, dim, along):
    ends, at = ([], 0)
    for a in arrays[:-1]:
        at += a.shape[along]
        ends.append(at)
    both = jnp.concatenate(arrays, axis=along)
    return tuple(jnp.split(lax.all_gather(both, axis, axis=dim, tiled=True), ends, axis=along))


def from_everyone(value, axis):
    copies = jnp.broadcast_to(value, (lax.axis_size(axis), *value.shape))
    return lax.all_to_all(copies, axis, split_axis=0, concat_axis=0, tiled=True)


def over_copies(value, axis):
    return from_everyone(value, axis).astype(jnp.float32).sum(axis=0)


def rotate(values, place, sign):
    width = values.shape[-1]
    half = width // 2
    rates = jnp.exp(jnp.arange(half, dtype=jnp.float32) * (-2.0 * math.log(10000.0) / width))
    angles = place.astype(jnp.float32)[:, None] * rates[None, :]
    cosine = jnp.cos(angles)[:, None, :]
    sine = sign * jnp.sin(angles)[:, None, :]
    first = values[..., :half]
    second = values[..., half:]
    return jnp.concatenate(
        [first * cosine - second * sine, second * cosine + first * sine], axis=-1
    )


def layout(segments, skips, documents):
    count = segments.shape[0]
    labels = jnp.arange(documents, dtype=jnp.int32)
    member = segments[:, None] == labels[None, :]
    starts = jnp.sum((segments[:, None] < labels[None, :]).astype(jnp.int32), axis=0)
    place = jnp.arange(count, dtype=jnp.int32) - jnp.sum(
        jnp.where(member, starts[None, :], 0), axis=1
    )
    keep = 1.0 - jnp.sum(jnp.where(member, skips[None, :], 0), axis=1).astype(jnp.float32)
    return (place, place // BLOCK, keep)


def unit_scale(values):
    factor = lax.rsqrt(jnp.mean(values * values, axis=1, keepdims=True) + EPSILON)
    return (values * factor, factor)


def to_rows(values, groups, share):
    count = values.shape[0]
    return (
        values.reshape(count, groups, share, HD)
        .transpose(1, 2, 0, 3)
        .reshape(groups, share * count, HD)
    )


def from_rows(values, groups, share):
    count = values.shape[1] // share
    return (
        values.reshape(groups, share, count, HD)
        .transpose(2, 0, 1, 3)
        .reshape(count, groups * share * HD)
    )


def permitted(query_seg, query_block, key_seg, key_block, share):
    table = (query_seg[:, None] == key_seg[None, :]) & (key_block[None, :] <= query_block[:, None])
    return jnp.tile(table, (share, 1))[None]


def project_heads(normed, query_weight, key_weight, value_weight, place):
    count = normed.shape[0]
    raw_query = jnp.dot(normed, query_weight, preferred_element_type=jnp.float32)
    raw_key = jnp.dot(normed, key_weight, preferred_element_type=jnp.float32)
    raw_value = jnp.dot(normed, value_weight, preferred_element_type=jnp.float32)
    query = (
        rotate(raw_query.reshape(count, -1, HD), place, 1.0).astype(jnp.bfloat16).reshape(count, -1)
    )
    key = rotate(raw_key.reshape(count, -1, HD), place, 1.0).astype(jnp.bfloat16).reshape(count, -1)
    return (query, key, raw_value.astype(jnp.bfloat16))


def fetch_forward(rows_shards, cols_shards):
    gathered_rows = in_one_piece(
        (
            rows_shards[0],
            rows_shards[1],
            rows_shards[2],
            rows_shards[3],
            rows_shards[4],
            rows_shards[5],
            rows_shards[6],
        ),
        DP,
        0,
        1,
    )
    gathered_cols = gather_turned((cols_shards[0], cols_shards[1]), DP, (1, 1))
    return (gathered_rows, gathered_cols)


def reduce_grads(row_grads, col_grads):
    owned_rows = jax.tree.map(
        lambda part: part.astype(jnp.float32),
        jax.tree.map(lambda part: summed_rows(part, DP, 0), for_sending(row_grads)),
    )
    owned_cols = jax.tree.map(
        lambda part: part.astype(jnp.float32),
        lax.psum_scatter(for_sending(col_grads), DP, scatter_dimension=1, tiled=True),
    )
    return (owned_rows, owned_cols)


def on_device(
    tokens,
    segment_ids,
    skip_mask,
    norm1_gain,
    w_query,
    w_key,
    w_value,
    w_out,
    norm2_gain,
    w_gate,
    w_up,
    w_down,
    cotangent,
):
    batches = tokens.shape[0]
    local_tokens = tokens.shape[1]
    documents = skip_mask.shape[1]
    offset = lax.axis_index(DP) * local_tokens
    heads_here = w_query.shape[1] // HD
    groups = w_key.shape[1] // HD
    share = heads_here // groups
    scale = 1.0 / math.sqrt(HD)
    rows_shards = (norm1_gain, w_query, w_key, w_value, norm2_gain, w_gate, w_up)
    cols_shards = (w_out, w_down)
    forward_rows, forward_cols = fetch_forward(rows_shards, cols_shards)
    kept = []
    outputs = []
    for micro in range(batches):
        gain_one, query_weight, key_weight, value_weight, gain_two, gate_weight, up_weight = (
            forward_rows
        )
        out_weight, down_weight = forward_cols
        segment_seq = segment_ids[micro]
        place, blocks, keep = layout(segment_seq, skip_mask[micro], documents)
        here_place = lax.dynamic_slice_in_dim(place, offset, local_tokens)
        here_block = lax.dynamic_slice_in_dim(blocks, offset, local_tokens)
        here_seg = lax.dynamic_slice_in_dim(segment_seq, offset, local_tokens)
        here_keep = lax.dynamic_slice_in_dim(keep, offset, local_tokens)[:, None]
        inputs = tokens[micro].astype(jnp.float32)
        first_unit, first_factor = unit_scale(inputs)
        first_normed = (first_unit * gain_one.astype(jnp.float32)).astype(jnp.bfloat16)
        queries, keys, values = project_heads(
            first_normed, query_weight, key_weight, value_weight, here_place
        )
        query_rows = to_rows(queries, groups, share)
        row_count = query_rows.shape[1]
        top = jnp.full((groups, row_count), NEGATIVE, jnp.float32)
        piece_key, piece_value = side_by_side((keys, values), DP, 0, 1)
        width = piece_key.shape[0]
        attend_allowed = permitted(here_seg, here_block, segment_seq, blocks, share)
        attend_key_heads = piece_key.reshape(width, groups, HD)
        attend_value_heads = piece_value.reshape(width, groups, HD)
        attend_scores = (
            jnp.einsum(
                "grd,ngd->grn", query_rows, attend_key_heads, preferred_element_type=jnp.float32
            )
            * scale
        )
        masked = jnp.where(attend_allowed, attend_scores, NEGATIVE)
        higher = jnp.maximum(top, jnp.max(masked, axis=2))
        weights = jnp.where(attend_allowed, jnp.exp(masked - higher[..., None]), 0.0)
        total = jnp.sum(weights, axis=2)
        running = jnp.einsum(
            "grn,ngd->grd",
            weights.astype(jnp.bfloat16),
            attend_value_heads,
            preferred_element_type=jnp.float32,
        )
        top, total, running = (higher, total, running)
        log_total = top + jnp.log(total)
        mixed_rows = (running / total[..., None]).astype(jnp.bfloat16)
        mixed_heads = from_rows(mixed_rows, groups, share)
        branch = over_copies(
            jnp.dot(mixed_heads, out_weight, preferred_element_type=jnp.float32).astype(
                jnp.bfloat16
            ),
            "mp",
        ).astype(jnp.float32)
        middle = inputs + here_keep * branch
        second_unit, second_factor = unit_scale(middle)
        second_normed = (second_unit * gain_two.astype(jnp.float32)).astype(jnp.bfloat16)
        gate = jnp.dot(second_normed, gate_weight, preferred_element_type=jnp.float32)
        up = jnp.dot(second_normed, up_weight, preferred_element_type=jnp.float32)
        hidden = (gate * jax.nn.sigmoid(gate) * up).astype(jnp.bfloat16)
        feedforward = over_copies(
            jnp.dot(hidden, down_weight, preferred_element_type=jnp.float32).astype(jnp.bfloat16),
            "mp",
        ).astype(jnp.float32)
        outputs.append((middle + here_keep * feedforward).astype(jnp.bfloat16))
        kept.append((mixed_rows, log_total, middle))
    backward_rows, backward_cols = (forward_rows, forward_cols)
    gathered_grads = None
    owned_grads = None
    input_grads = []
    for micro in range(batches):
        gain_one, query_weight, key_weight, value_weight, gain_two, gate_weight, up_weight = (
            backward_rows
        )
        out_weight, down_weight = backward_cols
        mixed_rows, log_total, middle = kept[micro]
        mixed_heads = from_rows(mixed_rows, groups, share)
        segment_seq = segment_ids[micro]
        place, blocks, keep = layout(segment_seq, skip_mask[micro], documents)
        here_place = lax.dynamic_slice_in_dim(place, offset, local_tokens)
        here_block = lax.dynamic_slice_in_dim(blocks, offset, local_tokens)
        here_seg = lax.dynamic_slice_in_dim(segment_seq, offset, local_tokens)
        here_keep = lax.dynamic_slice_in_dim(keep, offset, local_tokens)[:, None]
        inputs = tokens[micro].astype(jnp.float32)
        upstream = cotangent[micro].astype(jnp.float32)
        first_unit, first_factor = unit_scale(inputs)
        first_normed = (first_unit * gain_one.astype(jnp.float32)).astype(jnp.bfloat16)
        second_unit, second_factor = unit_scale(middle)
        second_normed = (second_unit * gain_two.astype(jnp.float32)).astype(jnp.bfloat16)
        gate = jnp.dot(second_normed, gate_weight, preferred_element_type=jnp.float32)
        up = jnp.dot(second_normed, up_weight, preferred_element_type=jnp.float32)
        sigmoid = jax.nn.sigmoid(gate)
        activated = gate * sigmoid
        hidden = (activated * up).astype(jnp.bfloat16)
        ffn_grad = (here_keep * upstream).astype(jnp.bfloat16)
        down_grad = jnp.einsum("tf,td->fd", hidden, ffn_grad, preferred_element_type=jnp.float32)
        hidden_grad = jnp.einsum(
            "td,fd->tf", ffn_grad, down_weight, preferred_element_type=jnp.float32
        )
        gate_grad = (hidden_grad * up * sigmoid * (1.0 + gate * (1.0 - sigmoid))).astype(
            jnp.bfloat16
        )
        up_grad = (hidden_grad * activated).astype(jnp.bfloat16)
        gate_weight_grad = jnp.einsum(
            "td,tf->df", second_normed, gate_grad, preferred_element_type=jnp.float32
        )
        up_weight_grad = jnp.einsum(
            "td,tf->df", second_normed, up_grad, preferred_element_type=jnp.float32
        )
        second_partial = jnp.einsum(
            "tf,df->td", gate_grad, gate_weight, preferred_element_type=jnp.float32
        ) + jnp.einsum("tf,df->td", up_grad, up_weight, preferred_element_type=jnp.float32)
        second_grad = over_copies(second_partial.astype(jnp.bfloat16), "mp").astype(jnp.float32)
        gain_two_grad = jnp.sum(second_grad * second_unit, axis=0)
        scaled_two = second_grad * gain_two.astype(jnp.float32)
        middle_grad = upstream + second_factor * (
            scaled_two - second_unit * jnp.mean(scaled_two * second_unit, axis=1, keepdims=True)
        )
        branch_grad = (here_keep * middle_grad).astype(jnp.bfloat16)
        out_weight_grad = jnp.einsum(
            "th,td->hd", mixed_heads, branch_grad, preferred_element_type=jnp.float32
        )
        heads_grad = jnp.einsum(
            "td,hd->th", branch_grad, out_weight, preferred_element_type=jnp.float32
        ).astype(jnp.bfloat16)
        grad_rows_heads = to_rows(heads_grad, groups, share)
        delta = jnp.sum(
            grad_rows_heads.astype(jnp.float32) * mixed_rows.astype(jnp.float32), axis=2
        )
        queries, keys, values = project_heads(
            first_normed, query_weight, key_weight, value_weight, here_place
        )
        query_rows = to_rows(queries, groups, share)
        keys_all, values_all = side_by_side((keys, values), DP, 0, 1)
        every = keys_all.shape[0]
        key_heads = keys_all.reshape(every, groups, HD)
        value_heads = values_all.reshape(every, groups, HD)
        allowed = permitted(here_seg, here_block, segment_seq, blocks, share)
        scores = (
            jnp.einsum("grd,ngd->grn", query_rows, key_heads, preferred_element_type=jnp.float32)
            * scale
        )
        probs = jnp.where(allowed, jnp.exp(scores - log_total[..., None]), 0.0)
        prob_grad = jnp.einsum(
            "grd,ngd->grn", grad_rows_heads, value_heads, preferred_element_type=jnp.float32
        )
        score_grad = (probs * (prob_grad - delta[..., None])).astype(jnp.bfloat16)
        query_grad_rows = (
            jnp.einsum("grn,ngd->grd", score_grad, key_heads, preferred_element_type=jnp.float32)
            * scale
        )
        key_grad_all = (
            jnp.einsum("grn,grd->ngd", score_grad, query_rows, preferred_element_type=jnp.float32)
            * scale
        )
        value_grad_all = jnp.einsum(
            "grn,grd->ngd",
            probs.astype(jnp.bfloat16),
            grad_rows_heads,
            preferred_element_type=jnp.float32,
        )
        stacked = jnp.concatenate(
            [key_grad_all.reshape(every, groups * HD), value_grad_all.reshape(every, groups * HD)],
            axis=1,
        )
        owned_kv = lax.psum_scatter(
            stacked.astype(jnp.bfloat16), DP, scatter_dimension=0, tiled=True
        ).astype(jnp.float32)
        key_grad = owned_kv[:, : groups * HD].reshape(local_tokens, groups, HD)
        value_pre = owned_kv[:, groups * HD :].astype(jnp.bfloat16)
        query_grad = from_rows(query_grad_rows, groups, share).reshape(local_tokens, heads_here, HD)
        query_pre = (
            rotate(query_grad, here_place, -1.0).reshape(local_tokens, -1).astype(jnp.bfloat16)
        )
        key_pre = rotate(key_grad, here_place, -1.0).reshape(local_tokens, -1).astype(jnp.bfloat16)
        query_weight_grad = jnp.einsum(
            "td,th->dh", first_normed, query_pre, preferred_element_type=jnp.float32
        )
        key_weight_grad = jnp.einsum(
            "td,th->dh", first_normed, key_pre, preferred_element_type=jnp.float32
        )
        value_weight_grad = jnp.einsum(
            "td,th->dh", first_normed, value_pre, preferred_element_type=jnp.float32
        )
        first_partial = jnp.einsum(
            "th,dh->td", query_pre, query_weight, preferred_element_type=jnp.float32
        )
        first_partial = first_partial + jnp.einsum(
            "th,dh->td", key_pre, key_weight, preferred_element_type=jnp.float32
        )
        first_partial = first_partial + jnp.einsum(
            "th,dh->td", value_pre, value_weight, preferred_element_type=jnp.float32
        )
        first_grad = over_copies(first_partial.astype(jnp.bfloat16), "mp").astype(jnp.float32)
        gain_one_grad = jnp.sum(first_grad * first_unit, axis=0)
        scaled_one = first_grad * gain_one.astype(jnp.float32)
        input_grad = middle_grad + first_factor * (
            scaled_one - first_unit * jnp.mean(scaled_one * first_unit, axis=1, keepdims=True)
        )
        input_grads.append(input_grad.astype(jnp.bfloat16))
        row_grads = (
            gain_one_grad,
            query_weight_grad,
            key_weight_grad,
            value_weight_grad,
            gain_two_grad,
            gate_weight_grad,
            up_weight_grad,
        )
        col_grads = (out_weight_grad, down_grad)
        local_grads = (row_grads, col_grads)
        gathered_grads = (
            local_grads
            if gathered_grads is None
            else jax.tree.map(jnp.add, gathered_grads, local_grads)
        )
    owned_grads = reduce_grads(gathered_grads[0], gathered_grads[1])
    owned_rows, owned_cols = owned_grads
    return (
        jnp.stack(outputs),
        jnp.stack(input_grads),
        owned_rows[0],
        owned_rows[1],
        owned_rows[2],
        owned_rows[3],
        owned_cols[0],
        owned_rows[4],
        owned_rows[5],
        owned_rows[6],
        owned_cols[1],
    )


def solution(mesh):
    split = Mesh(mesh.devices.reshape(4, 4, 2, mesh.shape["mp"]), ("dp_0", "dp_1", "dp_2", "mp"))
    in_specs = (
        P(None, DP, None),
        P(),
        P(),
        P(DP),
        P(DP, "mp"),
        P(DP, "mp"),
        P(DP, "mp"),
        P("mp", DP),
        P(DP),
        P(DP, "mp"),
        P(DP, "mp"),
        P("mp", DP),
        P(None, DP, None),
    )
    out_specs = (
        P(None, DP, None),
        P(None, DP, None),
        P(DP),
        P(DP, "mp"),
        P(DP, "mp"),
        P(DP, "mp"),
        P("mp", DP),
        P(DP),
        P(DP, "mp"),
        P(DP, "mp"),
        P("mp", DP),
    )
    return jax.shard_map(
        on_device, mesh=split, in_specs=in_specs, out_specs=out_specs, check_vma=False
    )
```

profile of v0, /device:TPU:1, one launch (start us, length us, event | category | flops | bytes accessed | tf_op | source)
XLA Modules:
  0.0 1739.0 jit_solution(18123388012324723272)
XLA Ops:
  15.0 146.5 %all-gather.5.cloned.1.call-done = bf16[2048,3586]{1,0:T(8,128)(2,1)} async-done(((bf16[64,3586]{1,0:T(8,128)(2,1)}), bf16[2048,3586]{1,0:T(8,128)(2,1)}) %all-gather.5.cloned.1.call-update) | async-done | bytes 14688272 | tf_op jit(solution)/shard_map/all_gather | solution.py:21
  176.3 4.3 slice_bitcast_fusion
  180.6 4.0 copy.53
  187.1 54.7 %all-gather.7.cloned.1.call-done = bf16[4096,256]{0,1:T(8,128)(2,1)} async-done(((bf16[128,256]{0,1:T(8,128)(2,1)}), bf16[4096,256]{0,1:T(8,128)(2,1)}) %all-gather.7.cloned.1.call-update) | async-done | bytes 2097168 | tf_op jit(solution)/shard_map/all_gather | solution.py:56
  249.8 94.4 %all-gather.9.cloned.1.call-done = bf16[2048,1920]{1,0:T(8,128)(2,1)} async-done(((bf16[64,1920]{1,0:T(8,128)(2,1)}), bf16[2048,1920]{1,0:T(8,128)(2,1)}) %all-gather.9.cloned.1.call-update) | async-done | bytes 7864336 | tf_op jit(solution)/shard_map/all_gather | solution.py:32
  348.2 6.0 all-to-all-start
  356.9 62.3 %all-gather.11.cloned.1.call-done = bf16[4096,256]{0,1:T(8,128)(2,1)} async-done(((bf16[128,256]{0,1:T(8,128)(2,1)}), bf16[4096,256]{0,1:T(8,128)(2,1)}) %all-gather.11.cloned.1.call-update) | async-done | bytes 2097168 | tf_op jit(solution)/shard_map/all_gather | solution.py:56
  431.8 5.7 all-to-all-start.2
  438.1 4.5 fusion.16
  445.7 16.6 all-to-all-done.2
  464.6 3.3 multiply_reduce_fusion.5
  468.1 5.0 fusion.28
  473.1 6.0 multiply_convert_fusion.9
  485.3 5.3 all-to-all-start.4
  490.6 4.8 fusion.14
  495.4 8.2 fusion.2
  504.3 11.3 all-to-all-done.4
  517.7 3.4 multiply_reduce_fusion.1
  526.7 3.1 fusion.10
  529.8 4.8 multiply_convert_fusion.1
  536.4 5.1 fusion.26
  541.6 3.2 multiply_convert_fusion.7
  551.3 5.3 all-to-all-start.6
  559.3 4.1 copy.62
  563.5 8.0 fusion.3
  571.5 13.1 all-to-all-done.6
  593.1 3.1 fusion.11
  596.2 4.7 multiply_convert_fusion
  605.1 4.1 copy.64
  609.2 3.8 convolution_multiply_fusion.3
  616.0 3.7 convolution_multiply_fusion.2
  620.1 4.3 add_convert_fusion.4
  624.7 104.3 %reduce-scatter.58.cloned.1.call-done = bf16[128,256]{1,0:T(8,128)(2,1)} async-done(((bf16[4096,256]{1,0:T(8,128)(2,1)}), bf16[128,256]{1,0:T(8,128)(2,1)}) %reduce-scatter.58.cloned.1.call-update) | async-done | bytes 65552
  732.0 182.4 %reduce-scatter.60.cloned.1.call-done = bf16[128,256]{1,0:T(8,128)(2,1)} async-done(((bf16[4096,256]{1,0:T(8,128)(2,1)}), bf16[128,256]{1,0:T(8,128)(2,1)}) %reduce-scatter.60.cloned.1.call-update) | async-done | bytes 65552
  922.7 4.2 add_convert_fusion.2
  927.0 37.8 %reduce-scatter.24.cloned.1.call-done = bf16[512,512]{1,0:T(8,128)(2,1)} async-done(((bf16[2048,512]{1,0:T(8,128)(2,1)}), bf16[512,512]{1,0:T(8,128)(2,1)}) %reduce-scatter.24.cloned.1.call-update) | async-done | bytes 524304 | tf_op jit(solution)/shard_map/reduce_scatter | solution.py:46
  964.9 22.0 %reduce-scatter.36.cloned.1.call-done = bf16[512,128]{1,0:T(8,128)(2,1)} async-done(((bf16[2048,128]{1,0:T(8,128)(2,1)}), bf16[512,128]{1,0:T(8,128)(2,1)}) %reduce-scatter.36.cloned.1.call-update) | async-done | bytes 131088 | tf_op jit(solution)/shard_map/reduce_scatter | solution.py:46
  987.0 7.0 fusion.269
  994.0 17.3 reduce-scatter.30.cloned.1.call-done
  1011.3 8.5 add_convert_fusion.1
  1020.8 4.6 fusion.48
  1027.1 7.8 all-to-all-start.1
  1034.9 4.7 fusion.51
  1039.6 20.2 %all-to-all-done.1 = bf16[4,128,2048]{2,1,0:T(8,128)(2,1)} async-done(((bf16[4,128,2048]{2,1,0:T(8,128)(2,1)}), bf16[4,128,2048]{2,1,0:T(8,128)(2,1)}, u32[]{:S(2)}, u32[]{:S(2)}) %all-to-all-start.1) | async-done | bytes 2097184 | tf_op jit(solution)/shard_map/all_to_all | solution.py:61
  1061.4 5.3 all-to-all-start.3
  1070.0 4.9 reduce-scatter.44.cloned.1.call-done
  1078.3 13.3 all-to-all-done.3
  1093.3 5.3 all-to-all-start.7
  1104.8 18.7 %all-to-all-done.7 = bf16[4,128,2048]{2,1,0:T(8,128)(2,1)} async-done(((bf16[4,128,2048]{2,1,0:T(8,128)(2,1)}), bf16[4,128,2048]{2,1,0:T(8,128)(2,1)}, u32[]{:S(2)}, u32[]{:S(2)}) %all-to-all-start.7) | async-done | bytes 2097184 | tf_op jit(solution)/shard_map/all_to_all | solution.py:61
  1125.1 5.3 all-to-all-start.5
  1137.2 3.9 reduce-scatter.32.cloned.1.call-done
  1144.2 61.2 %reduce-scatter.50.cloned.1.call-done = bf16[512,1408]{1,0:T(8,128)(2,1)} async-done(((bf16[2048,1408]{1,0:T(8,128)(2,1)}), bf16[512,1408]{1,0:T(8,128)(2,1)}) %reduce-scatter.50.cloned.1.call-update) | async-done | bytes 1441808 | tf_op jit(solution)/shard_map/reduce_scatter | solution.py:46
  1217.9 4.3 add_convert_fusion
  1222.3 8.7 reduce-scatter.46.cloned.1.call-done
  1234.8 13.9 reduce-scatter.28.cloned.1.call-done
  1250.2 13.6 reduce-scatter.40.cloned.1.call-done
  1265.2 14.2 reduce-scatter.34.cloned.1.call-done
  1280.8 8.8 all-reduce.7
  1289.7 9.6 all-reduce.6
  1299.4 5.3 all-reduce.8
  1309.0 166.1 %reduce-scatter.42.cloned.1.call-done = bf16[512,64]{0,1:T(8,128)(2,1)} async-done(((bf16[512,2048]{0,1:T(8,128)(2,1)}), bf16[512,64]{0,1:T(8,128)(2,1)}) %reduce-scatter.42.cloned.1.call-update) | async-done | bytes 65552 | tf_op jit(solution)/shard_map/reduce_scatter | solution.py:160
  1476.5 197.6 %reduce-scatter.56.cloned.1.call-done = bf16[1408,64]{0,1:T(8,128)(2,1)} async-done(((bf16[1408,2048]{0,1:T(8,128)(2,1)}), bf16[1408,64]{0,1:T(8,128)(2,1)}) %reduce-scatter.56.cloned.1.call-update) | async-done | bytes 180240 | tf_op jit(solution)/shard_map/reduce_scatter | solution.py:160
  1675.7 36.2 %reduce-scatter.48.cloned.1.call-done = bf16[64,1408]{1,0:T(8,128)(2,1)} async-done(((bf16[128,1408]{1,0:T(8,128)(2,1)}), bf16[64,1408]{1,0:T(8,128)(2,1)}) %reduce-scatter.48.cloned.1.call-update) | async-done | bytes 180240 | tf_op jit(solution)/shard_map/reduce_scatter | solution.py:46
  1713.6 16.9 reduce-scatter.54.cloned.1.call-done
  (415 shorter events, 170.7 us)
Async XLA Ops:
  7.2 160.6 %copy-start.2 = (bf16[2,128,2048]{2,1,0:T(8,128)(2,1)S(1)}, bf16[2,128,2048]{2,1,0:T(8,128)(2,1)}, u32[]{:S(2)}) copy-start(bf16[2,128,2048]{2,1,0:T(8,128)(2,1)} %param.13) | copy-start | bytes 3145732
  7.2 163.3 %copy-start.49 = (bf16[1408,64]{0,1:T(8,128)(2,1)S(1)}, bf16[1408,64]{0,1:T(8,128)(2,1)}, u32[]{:S(2)}) copy-start(bf16[1408,64]{0,1:T(8,128)(2,1)} %param.24) | copy-start | bytes 540676
  7.2 163.3 %copy-start.59 = (bf16[512,64]{0,1:T(8,128)(2,1)S(1)}, bf16[512,64]{0,1:T(8,128)(2,1)}, u32[]{:S(2)}) copy-start(bf16[512,64]{0,1:T(8,128)(2,1)} %param.20) | copy-start | bytes 196612
  7.2 154.3 %all-gather.5.cloned.1.call-start = ((), (), s32[]{:S(2)}) async-start(), calls=%async_computation.27 | async-start | bytes 15679488 | tf_op jit(solution)/shard_map/all_gather | solution.py:21
  11.1 230.7 %all-gather.7.cloned.1.call-start = ((), (), s32[]{:S(2)}) async-start(), calls=%async_computation.28 | async-start | bytes 2162688 | tf_op jit(solution)/shard_map/all_gather | solution.py:56
  11.2 164.6 %copy-start.83 = (f32[64]{0:T(128)}, f32[64]{0:T(128)S(1)}, u32[]{:S(2)}) copy-start(f32[64]{0:T(128)S(1)} %multiply_exponential_fusion) | copy-start | bytes 772
  13.2 163.0 %copy-start.85 = (f32[128]{0:T(128)}, f32[128]{0:T(128)S(1)}, u32[]{:S(2)}) copy-start(f32[128]{0:T(128)S(1)} %dynamic-slice_convert_fusion.5) | copy-start | bytes 1540
  13.5 162.8 %copy-start.87 = (f32[128]{0:T(128)}, f32[128]{0:T(128)S(1)}, u32[]{:S(2)}) copy-start(f32[128]{0:T(128)S(1)} %dynamic-slice_convert_fusion.4) | copy-start | bytes 1540
  15.0 169.6 %copy-start.65 = (f32[128]{0:T(128)}, f32[128]{0:T(128)S(1)}, u32[]{:S(2)}) copy-start(f32[128]{0:T(128)S(1)} %get-tuple-element.106) | copy-start | bytes 1540
  15.0 339.3 %copy-start.62 = (f32[128]{0:T(128)}, f32[128]{0:T(128)S(1)}, u32[]{:S(2)}) copy-start(f32[128]{0:T(128)S(1)} %get-tuple-element.105) | copy-start | bytes 1540
  170.4 173.8 %all-gather.9.cloned.1.call-start = ((), (), s32[]{:S(2)}) async-start(), calls=%async_computation.29 | async-start | bytes 8110080 | tf_op jit(solution)/shard_map/all_gather | solution.py:32
  171.2 248.0 %all-gather.11.cloned.1.call-start = ((), (), s32[]{:S(2)}) async-start(), calls=%async_computation.30 | async-start | bytes 2162688 | tf_op jit(solution)/shard_map/all_gather | solution.py:56
  174.7 247.5 %copy-start.12 = (pred[128,4096]{1,0:T(8,128)(4,1)}, pred[128,4096]{1,0:T(8,128)(4,1)S(1)}, u32[]{:S(2)}) copy-start(pred[128,4096]{1,0:T(8,128)(4,1)S(1)} %compare_and_fusion) | copy-start | bytes 1572868
  175.7 180.9 %copy-start.45 = (f32[128,64]{0,1:T(8,128)}, f32[128,64]{0,1:T(8,128)S(1)}, u32[]{:S(2)}) copy-start(f32[128,64]{0,1:T(8,128)S(1)} %get-tuple-element.95) | copy-start | bytes 98308
  176.2 68.6 %copy-start.13 = (pred[128,4096]{1,0:T(8,128)(4,1)}, pred[128,4096]{1,0:T(8,128)(4,1)S(1)}, u32[]{:S(2)}) copy-start(pred[128,4096]{1,0:T(8,128)(4,1)S(1)} %compare_and_fusion.1) | copy-start | bytes 1572868
  248.4 99.8 %copy-start.74 = (f32[512]{0:T(512)}, f32[512]{0:T(512)S(1)}, u32[]{:S(2)}) copy-start(f32[512]{0:T(512)S(1)} %get-tuple-element.47) | copy-start | bytes 6148
  249.7 94.5 %copy-start.35 = (bf16[512,128]{1,0:T(8,128)(2,1)}, bf16[512,128]{1,0:T(8,128)(2,1)S(1)}, u32[]{:S(2)}) copy-start(bf16[512,128]{1,0:T(8,128)(2,1)S(1)} %fusion.96) | copy-start | bytes 393220
  348.2 82.0 %all-to-all-start = ((bf16[4,128,2048]{2,1,0:T(8,128)(2,1)}), bf16[4,128,2048]{2,1,0:T(8,128)(2,1)}, u32[]{:S(2)}, u32[]{:S(2)}) async-start(bf16[4,128,2048]{2,1,0:T(8,128)(2,1)} %broadcast_in_dim.83), calls=%async_computation | async-start | bytes 4194304 | tf_op jit(solution)/shard_map/all_to_all | solution.py:61
  427.7 14.9 copy-start.31
  431.8 30.6 %all-to-all-start.2 = ((bf16[4,128,2048]{2,1,0:T(8,128)(2,1)}), bf16[4,128,2048]{2,1,0:T(8,128)(2,1)}, u32[]{:S(2)}, u32[]{:S(2)}) async-start(bf16[4,128,2048]{2,1,0:T(8,128)(2,1)} %broadcast_in_dim.88), calls=%async_computation.2 | async-start | bytes 4194304 | tf_op jit(solution)/shard_map/all_to_all | solution.py:61
  462.3 16.7 slice-start
  485.3 30.2 %all-to-all-start.4 = ((bf16[4,128,2048]{2,1,0:T(8,128)(2,1)}), bf16[4,128,2048]{2,1,0:T(8,128)(2,1)}, u32[]{:S(2)}, u32[]{:S(2)}) async-start(bf16[4,128,2048]{2,1,0:T(8,128)(2,1)} %broadcast_in_dim.90), calls=%async_computation.4 | async-start | bytes 4194304 | tf_op jit(solution)/shard_map/all_to_all | solution.py:61
  526.7 14.9 slice-start.4
  551.3 33.3 %all-to-all-start.6 = ((bf16[4,128,2048]{2,1,0:T(8,128)(2,1)}), bf16[4,128,2048]{2,1,0:T(8,128)(2,1)}, u32[]{:S(2)}, u32[]{:S(2)}) async-start(bf16[4,128,2048]{2,1,0:T(8,128)(2,1)} %broadcast_in_dim.92), calls=%async_computation.6 | async-start | bytes 4194304 | tf_op jit(solution)/shard_map/all_to_all | solution.py:61
  556.6 172.4 %reduce-scatter.58.cloned.1.call-start = ((), (), s32[]{:S(2)}) async-start(), calls=%async_computation.48 | async-start | bytes 2162688
  563.4 351.0 %reduce-scatter.60.cloned.1.call-start = ((), (), s32[]{:S(2)}) async-start(), calls=%async_computation.49 | async-start | bytes 2162688
  563.5 23.2 %copy-start.8 = (f32[128,2048]{1,0:T(8,128)S(1)}, f32[128,2048]{1,0:T(8,128)}, u32[]{:S(2)}) copy-start(f32[128,2048]{1,0:T(8,128)} %get-tuple-element.60) | copy-start | bytes 3145732
  571.5 21.4 %copy-start.34 = (bf16[512,128]{1,0:T(8,128)(2,1)S(1)}, bf16[512,128]{1,0:T(8,128)(2,1)}, u32[]{:S(2)}) copy-start(bf16[512,128]{1,0:T(8,128)(2,1)} %copy-done.33) | copy-start | bytes 393220
  609.2 355.7 %reduce-scatter.24.cloned.1.call-start = ((), (), s32[]{:S(2)}) async-start(), calls=%async_computation.31 | async-start | bytes 2621440 | tf_op jit(solution)/shard_map/reduce_scatter | solution.py:46
  620.0 297.8 %copy-start.84 = (f32[64]{0:T(128)S(1)}, f32[64]{0:T(128)}, u32[]{:S(2)}) copy-start(f32[64]{0:T(128)} %copy-done.83) | copy-start | bytes 772
  620.0 297.8 %copy-start.86 = (f32[128]{0:T(128)S(1)}, f32[128]{0:T(128)}, u32[]{:S(2)}) copy-start(f32[128]{0:T(128)} %copy-done.85) | copy-start | bytes 1540
  620.0 297.8 %copy-start.88 = (f32[128]{0:T(128)S(1)}, f32[128]{0:T(128)}, u32[]{:S(2)}) copy-start(f32[128]{0:T(128)} %copy-done.87) | copy-start | bytes 1540
  624.4 295.6 %copy-start.16 = (bf16[128,2048]{1,0:T(8,128)(2,1)S(1)}, bf16[128,2048]{1,0:T(8,128)(2,1)}, u32[]{:S(2)}) copy-start(bf16[128,2048]{1,0:T(8,128)(2,1)} %copy-done.15) | copy-start | bytes 1572868
  624.4 362.5 %reduce-scatter.36.cloned.1.call-start = ((), (), s32[]{:S(2)}) async-start(), calls=%async_computation.37 | async-start | bytes 655360 | tf_op jit(solution)/shard_map/reduce_scatter | solution.py:46
  916.9 94.4 %reduce-scatter.30.cloned.1.call-start = ((), (), s32[]{:S(2)}) async-start(), calls=%async_computation.34 | async-start | bytes 655360 | tf_op jit(solution)/shard_map/reduce_scatter | solution.py:46
  919.9 155.0 %reduce-scatter.44.cloned.1.call-start = ((), (), s32[]{:S(2)}) async-start(), calls=%async_computation.41 | async-start | bytes 7208960 | tf_op jit(solution)/shard_map/reduce_scatter | solution.py:46
  927.0 203.4 %reduce-scatter.26.cloned.1.call-start = ((), (), s32[]{:S(2)}) async-start(), calls=%async_computation.32 | async-start | bytes 655360 | tf_op jit(solution)/shard_map/reduce_scatter | solution.py:46
  964.9 169.2 %reduce-scatter.38.cloned.1.call-start = ((), (), s32[]{:S(2)}) async-start(), calls=%async_computation.38 | async-start | bytes 163840 | tf_op jit(solution)/shard_map/reduce_scatter | solution.py:46
  986.9 154.2 %reduce-scatter.32.cloned.1.call-start = ((), (), s32[]{:S(2)}) async-start(), calls=%async_computation.35 | async-start | bytes 163840 | tf_op jit(solution)/shard_map/reduce_scatter | solution.py:46
  1011.3 194.1 %reduce-scatter.50.cloned.1.call-start = ((), (), s32[]{:S(2)}) async-start(), calls=%async_computation.44 | async-start | bytes 7208960 | tf_op jit(solution)/shard_map/reduce_scatter | solution.py:46
  1027.1 32.8 %all-to-all-start.1 = ((bf16[4,128,2048]{2,1,0:T(8,128)(2,1)}), bf16[4,128,2048]{2,1,0:T(8,128)(2,1)}, u32[]{:S(2)}, u32[]{:S(2)}) async-start(bf16[4,128,2048]{2,1,0:T(8,128)(2,1)} %broadcast_in_dim.84), calls=%async_computation.1 | async-start | bytes 4194304 | tf_op jit(solution)/shard_map/all_to_all | solution.py:61
  1061.4 30.2 %all-to-all-start.3 = ((bf16[4,128,2048]{2,1,0:T(8,128)(2,1)}), bf16[4,128,2048]{2,1,0:T(8,128)(2,1)}, u32[]{:S(2)}, u32[]{:S(2)}) async-start(bf16[4,128,2048]{2,1,0:T(8,128)(2,1)} %broadcast_in_dim.89), calls=%async_computation.3 | async-start | bytes 4194304 | tf_op jit(solution)/shard_map/all_to_all | solution.py:61
  1066.7 164.3 %reduce-scatter.46.cloned.1.call-start = ((), (), s32[]{:S(2)}) async-start(), calls=%async_computation.42 | async-start | bytes 1802240 | tf_op jit(solution)/shard_map/reduce_scatter | solution.py:46
  1076.6 24.8 %copy-start.52 = (bf16[128,1,64]{0,2,1:T(8,128)(2,1)S(1)}, bf16[128,1,64]{0,2,1:T(8,128)(2,1)}, u32[]{:S(2)}) copy-start(bf16[128,1,64]{0,2,1:T(8,128)(2,1)} %copy-done.51) | copy-start | bytes 49156
  1076.6 24.8 %copy-start.54 = (bf16[128,1,64]{0,2,1:T(8,128)(2,1)S(1)}, bf16[128,1,64]{0,2,1:T(8,128)(2,1)}, u32[]{:S(2)}) copy-start(bf16[128,1,64]{0,2,1:T(8,128)(2,1)} %copy-done.53) | copy-start | bytes 49156
  1078.3 24.9 %copy-start.50 = (bf16[128,256]{1,0:T(8,128)(2,1)S(1)}, bf16[128,256]{1,0:T(8,128)(2,1)}, u32[]{:S(2)}) copy-start(bf16[128,256]{1,0:T(8,128)(2,1)} %reduce-scatter.58.cloned.1.call-done) | copy-start | bytes 196612
  1093.3 30.2 %all-to-all-start.7 = ((bf16[4,128,2048]{2,1,0:T(8,128)(2,1)}), bf16[4,128,2048]{2,1,0:T(8,128)(2,1)}, u32[]{:S(2)}, u32[]{:S(2)}) async-start(bf16[4,128,2048]{2,1,0:T(8,128)(2,1)} %broadcast_in_dim.93), calls=%async_computation.7 | async-start | bytes 4194304 | tf_op jit(solution)/shard_map/all_to_all | solution.py:61
  1125.1 80.4 %all-to-all-start.5 = ((bf16[4,128,2048]{2,1,0:T(8,128)(2,1)}), bf16[4,128,2048]{2,1,0:T(8,128)(2,1)}, u32[]{:S(2)}, u32[]{:S(2)}) async-start(bf16[4,128,2048]{2,1,0:T(8,128)(2,1)} %broadcast_in_dim.91), calls=%async_computation.5 | async-start | bytes 4194304 | tf_op jit(solution)/shard_map/all_to_all | solution.py:61
  1130.4 118.4 %reduce-scatter.28.cloned.1.call-start = ((), (), s32[]{:S(2)}) async-start(), calls=%async_computation.33 | async-start | bytes 196608 | tf_op jit(solution)/shard_map/reduce_scatter | solution.py:46
  1130.9 132.9 %reduce-scatter.40.cloned.1.call-start = ((), (), s32[]{:S(2)}) async-start(), calls=%async_computation.39 | async-start | bytes 49152 | tf_op jit(solution)/shard_map/reduce_scatter | solution.py:46
  1134.0 73.7 %copy-start.64 = (f32[128]{0:T(128)S(1)}, f32[128]{0:T(128)}, u32[]{:S(2)}) copy-start(f32[128]{0:T(128)} %copy-done.62) | copy-start | bytes 1540
  1134.0 73.8 %copy-start.67 = (f32[128]{0:T(128)S(1)}, f32[128]{0:T(128)}, u32[]{:S(2)}) copy-start(f32[128]{0:T(128)} %copy-done.65) | copy-start | bytes 1540
  1134.1 145.4 %reduce-scatter.34.cloned.1.call-start = ((), (), s32[]{:S(2)}) async-start(), calls=%async_computation.36 | async-start | bytes 49152 | tf_op jit(solution)/shard_map/reduce_scatter | solution.py:46
  1137.2 72.5 %copy-start.5 = (f32[128,2048]{1,0:T(8,128)S(1)}, f32[128,2048]{1,0:T(8,128)}, u32[]{:S(2)}) copy-start(f32[128,2048]{1,0:T(8,128)} %convert_reduce_fusion.7) | copy-start | bytes 3145732
  1137.2 72.5 %copy-start.79 = (f32[128]{0:T(128)S(1)}, f32[128]{0:T(128)}, u32[]{:S(2)}) copy-start(f32[128]{0:T(128)} %copy-done.77) | copy-start | bytes 1540
  1137.2 72.5 %copy-start.82 = (f32[128]{0:T(128)S(1)}, f32[128]{0:T(128)}, u32[]{:S(2)}) copy-start(f32[128]{0:T(128)} %copy-done.80) | copy-start | bytes 1540
  1137.2 72.6 %copy-start.91 = (f32[128]{0:T(128)S(1)}, f32[128]{0:T(128)}, u32[]{:S(2)}) copy-start(f32[128]{0:T(128)} %copy-done.90) | copy-start | bytes 1540
  1141.1 164.5 %reduce-scatter.52.cloned.1.call-start = ((), (), s32[]{:S(2)}) async-start(), calls=%async_computation.45 | async-start | bytes 1802240 | tf_op jit(solution)/shard_map/reduce_scatter | solution.py:46
  1205.4 269.6 %reduce-scatter.42.cloned.1.call-start = ((), (), s32[]{:S(2)}) async-start(), calls=%async_computation.40 | async-start | bytes 2162688 | tf_op jit(solution)/shard_map/reduce_scatter | solution.py:160
  1215.9 458.2 %reduce-scatter.56.cloned.1.call-start = ((), (), s32[]{:S(2)}) async-start(), calls=%async_computation.47 | async-start | bytes 5947392 | tf_op jit(solution)/shard_map/reduce_scatter | solution.py:160
  1222.2 84.7 %copy-start.30 = (bf16[1,128,2048]{2,1,0:T(8,128)(2,1)S(1)}, bf16[1,128,2048]{2,1,0:T(8,128)(2,1)}, u32[]{:S(2)}) copy-start(bf16[1,128,2048]{2,1,0:T(8,128)(2,1)} %get-tuple-element.35) | copy-start | bytes 1572868
  1222.2 85.7 %copy-start.29 = (bf16[1,128,2048]{2,1,0:T(8,128)(2,1)S(1)}, bf16[1,128,2048]{2,1,0:T(8,128)(2,1)}, u32[]{:S(2)}) copy-start(bf16[1,128,2048]{2,1,0:T(8,128)(2,1)} %get-tuple-element.51) | copy-start | bytes 1572868
  1222.2 489.7 %reduce-scatter.48.cloned.1.call-start = ((), (), s32[]{:S(2)}) async-start(), calls=%async_computation.43 | async-start | bytes 540672 | tf_op jit(solution)/shard_map/reduce_scatter | solution.py:46
  1231.0 499.6 %reduce-scatter.54.cloned.1.call-start = ((), (), s32[]{:S(2)}) async-start(), calls=%async_computation.46 | async-start | bytes 540672 | tf_op jit(solution)/shard_map/reduce_scatter | solution.py:46
  (75 other events, 415.0 us)
Sparse Core Ops, SparseCore 0:
  11.8 149.6 all-gather.4
  170.5 71.2 all-gather.6
  245.4 98.7 all-gather.8
  347.4 71.7 all-gather.10
  563.5 165.4 reduce-scatter.57
  731.3 183.0 reduce-scatter.59
  916.8 48.0 reduce-scatter.23
  967.4 19.4 reduce-scatter.35
  990.0 21.2 reduce-scatter.29
  1013.6 61.1 reduce-scatter.43
  1077.4 19.2 reduce-scatter.25
  1099.0 19.5 reduce-scatter.37
  1121.0 20.0 reduce-scatter.31
  1143.5 61.8 reduce-scatter.49
  1207.8 23.1 reduce-scatter.45
  1233.2 15.4 reduce-scatter.27
  1251.0 12.8 reduce-scatter.39
  1266.1 13.2 reduce-scatter.33
  1282.0 23.6 reduce-scatter.51
  1308.0 167.0 reduce-scatter.41
  1477.4 196.5 reduce-scatter.55
  1676.4 35.4 reduce-scatter.47
  1714.3 16.2 reduce-scatter.53
where the time goes:
time: 1750 us; the launch traced here: 1740 us
  waiting for transfers between devices  1350 us (77%)
  matrix products  163 us (9%)
  other arithmetic  85.7 us (5%)
  starting transfers between devices  47.8 us (3%)
  local copies, waits for them, and re-layouts  47.4 us (3%)
  blocking collectives  23.6 us (1%)
  between operations  18 us (1%)
    reduce_scatter x2, waiting for transfers between devices, reduce_grads(): lax.psum_scatter(for_sending(col_grads), DP, scatter_dimension=1, tiled=T...  364 us
    unnamed x25, waiting for transfers between devices  288 us
    reduce_scatter x15, waiting for transfers between devices, summed_rows(): value = lax.psum_scatter(value, axis, scatter_dimension=dim, tiled=True)  252 us
    all_gather x1, waiting for transfers between devices, in_one_piece(): filled, at, done = (lax.all_gather(both, axis, axis=dim, tiled=True), 0, [])  147 us
    all_gather x2, waiting for transfers between devices, side_by_side(): lax.all_gather(both, axis, axis=dim, tiled=True)  117 us
    all_gather x1, waiting for transfers between devices, gather_turned(): filled, at, done = (lax.all_gather(both, axis, axis=0, tiled=True), 0, [])  94.4 us
    all_to_all x8, waiting for transfers between devices, from_everyone(): return lax.all_to_all(copies, axis, split_axis=0, concat_axis=0, tiled=True)  93.2 us
    all_to_all x8, starting transfers between devices, from_everyone(): return lax.all_to_all(copies, axis, split_axis=0, concat_axis=0, tiled=True)  45.9 us
  transfers between devices with their start and end apart: 31, of which 27 were waited for; matrix products, arithmetic and copies ran while one was open for 12% of the time, Pallas kernels for 0%

commit v1 on v0

v1 whole, which is shorter than its diff:
```python
import math

import jax
import jax.numpy as jnp
from jax import lax
from jax.sharding import Mesh
from jax.sharding import PartitionSpec as P

HD = 128
BLOCK = 256
EPSILON = 1e-05
NEGATIVE = -1e30

AXES = ("z", "y", "xh", "xl", "c")
DP = ("z", "y", "xh")
MP = ("xl", "c")
ZY = ("z", "y")
X4 = ("xh", "xl")
F32 = jnp.float32
BF16 = jnp.bfloat16


def exchange(value, axes):
    return lax.all_to_all(value, axes, split_axis=0, concat_axis=0, tiled=True)


def from_everyone(value, axes):
    return exchange(jnp.broadcast_to(value, (lax.axis_size(axes), *value.shape)), axes)


def flip(value, axis):
    return lax.ppermute(value, axis, [(0, 1), (1, 0)])


def swap(value):
    return lax.ppermute(value, ("xh", "c"), [(1, 2), (2, 1)])


def pick(first, when, own, other):
    return jnp.where(when == 0, own, other) if first else jnp.where(when == 0, other, own)


def ordered(when, own, other, axis):
    return jnp.concatenate([pick(True, when, own, other), pick(False, when, own, other)], axis=axis)


def rope_tables(place, sign):
    half = HD // 2
    rates = jnp.exp(jnp.arange(half, dtype=F32) * (-2.0 * math.log(10000.0) / HD))
    angles = place.astype(F32)[:, None] * rates[None, :]
    return jnp.cos(angles)[:, None, :], sign * jnp.sin(angles)[:, None, :]


def rotate(values, cosine, sine):
    half = HD // 2
    first, second = values[..., :half], values[..., half:]
    return jnp.concatenate(
        [first * cosine - second * sine, second * cosine + first * sine], axis=-1
    )


def layout(segments, skips, documents):
    count = segments.shape[0]
    labels = jnp.arange(documents, dtype=jnp.int32)
    member = segments[:, None] == labels[None, :]
    starts = jnp.sum((segments[:, None] < labels[None, :]).astype(jnp.int32), axis=0)
    place = jnp.arange(count, dtype=jnp.int32) - jnp.sum(
        jnp.where(member, starts[None, :], 0), axis=1
    )
    keep = 1.0 - jnp.sum(jnp.where(member, skips[None, :], 0), axis=1).astype(F32)
    return place, place // BLOCK, keep


def unit_scale(values):
    factor = lax.rsqrt(jnp.mean(values * values, axis=1, keepdims=True) + EPSILON)
    return values * factor, factor


def dot(a, b, dims):
    return lax.dot_general(a, b, (dims, ((), ())), preferred_element_type=F32)


def spread(piece, xl, core):
    both = ordered(xl, piece, flip(piece, "xl"), 0)
    return ordered(core, both[None], flip(both, "c")[None], 0)


def on_device(
    tokens,
    segment_ids,
    skip_mask,
    norm1_gain,
    w_query,
    w_key,
    w_value,
    w_out,
    norm2_gain,
    w_gate,
    w_up,
    w_down,
    cotangent,
):
    local, width = tokens.shape[1:]
    documents = skip_mask.shape[1]
    xh, xl, core = lax.axis_index("xh"), lax.axis_index("xl"), lax.axis_index("c")
    chip = lax.axis_index(X4)
    plane = lax.axis_index(ZY)
    planes = lax.axis_size(ZY)
    queries = 2 * local
    mine = queries // 4
    offset = plane * queries
    heads = w_query.shape[1] // HD
    wide = heads * HD
    scale = 1.0 / math.sqrt(HD)
    rows = w_query.shape[0]
    hidden_local = w_gate.shape[1]
    tiles = hidden_local // 128
    part = (tiles + 1) // 2 * 128
    lead = hidden_local - part
    spare = part - lead

    gain_one = norm1_gain.astype(F32)[:, None]
    gain_two = norm2_gain.astype(F32)[:, None]

    with jax.named_scope("attn_weights"):
        own_heads = jnp.concatenate(
            [
                (gain_one * w_query.astype(F32)).astype(BF16),
                (gain_one * w_key.astype(F32)).astype(BF16),
                (gain_one * w_value.astype(F32)).astype(BF16),
                w_out.T,
            ],
            axis=1,
        )
        half_heads = jnp.where(core == xh, own_heads, swap(own_heads))
        total_in = wide + 2 * HD
        half_in = from_everyone(half_heads[:, :total_in], ZY)
        half_out = from_everyone(half_heads[:, total_in:], ZY)

        def both_halves(half):
            other = flip(half, "c")
            pair = ordered(core, half[:, None], other[:, None], 1)
            return pair.reshape(width, half.shape[-1])

        weight_in = both_halves(half_in)
        weight_out = both_halves(half_out)

    with jax.named_scope("ffn_weights"):
        own_hidden = jnp.stack(
            [
                (gain_two * w_gate.astype(F32)).astype(BF16),
                (gain_two * w_up.astype(F32)).astype(BF16),
                w_down.T,
            ],
            axis=1,
        ).reshape(rows, 3, hidden_local)

        def columns(which):
            share = lax.dynamic_slice_in_dim(own_hidden, which * lead, part, axis=2)
            blank = (which == 1) & (lax.broadcasted_iota(jnp.int32, share.shape, 2) < spare)
            return jnp.where(blank, jnp.zeros_like(share), share).reshape(rows, 3 * part)

        pair_rows = ordered(xh, columns(xh), flip(columns(1 - xh), "xh"), 0)
        hidden_weight = lax.all_gather(pair_rows, ZY, axis=0, tiled=True)

    with jax.named_scope("layout"):
        segment_own = lax.dynamic_index_in_dim(segment_ids, core, 0, keepdims=False)
        segment_other = lax.dynamic_index_in_dim(segment_ids, 1 - core, 0, keepdims=False)
        skip_own = lax.dynamic_index_in_dim(skip_mask, core, 0, keepdims=False)
        skip_other = lax.dynamic_index_in_dim(skip_mask, 1 - core, 0, keepdims=False)
        place, blocks, keep = layout(segment_own, skip_own, documents)
        keep_other = layout(segment_other, skip_other, documents)[2]
        here = lambda a, at, n: lax.dynamic_slice_in_dim(a, at, n)
        here_place, here_block = here(place, offset, queries), here(blocks, offset, queries)
        here_seg = here(segment_own, offset, queries)
        keep_all = jnp.concatenate([here(keep, offset, queries), here(keep_other, offset, queries)])
        keep_mine = here(keep, offset + chip * mine, mine)[:, None]
        cosine, sine = rope_tables(here_place, 1.0)

    with jax.named_scope("first_norm"):
        tokens_own = lax.dynamic_index_in_dim(tokens, core, 0, keepdims=False)
        tokens_all = ordered(xh, tokens_own, flip(tokens_own, "xh"), 0)
        unit_all = unit_scale(tokens_all.astype(F32))[0].astype(BF16)
        x_mine = lax.dynamic_slice_in_dim(tokens_own, xl * mine, mine).astype(F32)
        first_unit, first_factor = unit_scale(x_mine)

    with jax.named_scope("cotangent"):
        grad_own = lax.dynamic_index_in_dim(cotangent, core, 0, keepdims=False)
        grad_all = ordered(xh, grad_own, flip(grad_own, "xh"), 0)
        grad_both = jnp.concatenate([grad_all, flip(grad_all, "c")], axis=0)
        ffn_grad = (keep_all[:, None] * grad_both.astype(F32)).astype(BF16)
        upstream = lax.dynamic_slice_in_dim(grad_own, xl * mine, mine).astype(F32)

    with jax.named_scope("project"):
        raw = dot(unit_all, weight_in, ((1,), (0,)))
        query = rotate(raw[:, :wide].reshape(queries, heads, HD), cosine, sine).astype(BF16)
        key = rotate(raw[:, wide : wide + HD].reshape(queries, 1, HD), cosine, sine)
        key_value = jnp.concatenate([key[:, 0], raw[:, wide + HD :]], axis=1).astype(BF16)
    with jax.named_scope("kv_gather"):
        everyone = from_everyone(key_value, ZY)
        every = planes * queries
        everyone = everyone.reshape(every, 2 * HD)
        keys, values = everyone[:, :HD], everyone[:, HD:]

    with jax.named_scope("attend"):
        allowed = (here_seg[:, None] == segment_own[None, :]) & (
            blocks[None, :] <= here_block[:, None]
        )
        query_rows = query.transpose(1, 0, 2)
        scores = jnp.einsum("hqd,nd->hqn", query_rows, keys, preferred_element_type=F32) * scale
        masked = jnp.where(allowed[None], scores, NEGATIVE)
        top = jnp.max(masked, axis=2)
        weights = jnp.where(allowed[None], jnp.exp(masked - top[..., None]), 0.0)
        total = jnp.sum(weights, axis=2)
        running = jnp.einsum("hqn,nd->hqd", weights.astype(BF16), values, preferred_element_type=F32)
        log_total = top + jnp.log(total)
        mixed_rows = (running / total[..., None]).astype(BF16)
        mixed = mixed_rows.transpose(1, 0, 2).reshape(queries, wide)

    with jax.named_scope("branch"):
        partial = dot(mixed, weight_out, ((1,), (1,))).astype(BF16)
        branch = exchange(partial.reshape(4, mine, width), X4).astype(F32).sum(axis=0)
        middle = x_mine + keep_mine * branch
        second_unit, second_factor = unit_scale(middle)
        unit_own = from_everyone(second_unit.astype(BF16), X4).reshape(queries, width)
        unit_both = jnp.concatenate([unit_own, flip(unit_own, "c")], axis=0)

    with jax.named_scope("ffn"):
        gate_weight = hidden_weight[:, :part]
        up_weight = hidden_weight[:, part : 2 * part]
        down_weight = hidden_weight[:, 2 * part :]
        gate = dot(unit_both, gate_weight, ((1,), (0,)))
        up = dot(unit_both, up_weight, ((1,), (0,)))
        sigmoid = jax.nn.sigmoid(gate)
        activated = gate * sigmoid
        hidden = (activated * up).astype(BF16)

        def own_sum(partial):
            sent = flip(partial[queries:].astype(BF16), "c")
            both = (partial[:queries] + sent.astype(F32)).astype(BF16)
            return exchange(both.reshape(4, mine, width), X4).astype(F32).sum(axis=0)

    with jax.named_scope("ffn_back"):
        hidden_grad = dot(ffn_grad, down_weight, ((1,), (0,)))
        gate_grad = (hidden_grad * up * sigmoid * (1.0 + gate * (1.0 - sigmoid))).astype(BF16)
        up_grad = (hidden_grad * activated).astype(BF16)
        scaled_two = own_sum(
            dot(gate_grad, gate_weight, ((1,), (1,))) + dot(up_grad, up_weight, ((1,), (1,)))
        )
        hidden_weight_grad = jnp.concatenate(
            [
                dot(unit_both, gate_grad, ((0,), (0,))).astype(BF16),
                dot(unit_both, up_grad, ((0,), (0,))).astype(BF16),
                dot(ffn_grad, hidden, ((0,), (0,))).astype(BF16),
            ],
            axis=1,
        )
        hidden_owned = lax.psum_scatter(hidden_weight_grad, ZY, scatter_dimension=0, tiled=True)
        gain_two_sum = jnp.sum(scaled_two * second_unit, axis=0)
        middle_grad = upstream + second_factor * (
            scaled_two - second_unit * jnp.mean(scaled_two * second_unit, axis=1, keepdims=True)
        )
        branch_grad = from_everyone((keep_mine * middle_grad).astype(BF16), X4)
        branch_grad = branch_grad.reshape(queries, width)

    with jax.named_scope("result"):
        feedforward = own_sum(dot(hidden, down_weight, ((1,), (1,))))
        result = spread((middle + keep_mine * feedforward).astype(BF16), xl, core)

    with jax.named_scope("attend_back"):
        mixed_grad = dot(branch_grad, weight_out, ((1,), (0,))).astype(BF16)
        out_weight_grad = dot(branch_grad, mixed, ((0,), (0,)))
        grad_rows = mixed_grad.reshape(queries, heads, HD).transpose(1, 0, 2)
        delta = jnp.sum(grad_rows.astype(F32) * mixed_rows.astype(F32), axis=2)
        probs = jnp.where(allowed[None], jnp.exp(scores - log_total[..., None]), 0.0)
        prob_grad = jnp.einsum("hqd,nd->hqn", grad_rows, values, preferred_element_type=F32)
        score_grad = (probs * (prob_grad - delta[..., None])).astype(BF16)
        query_grad = jnp.einsum("hqn,nd->qhd", score_grad, keys, preferred_element_type=F32) * scale
        key_grad = (
            jnp.einsum("hqn,hqd->nd", score_grad, query_rows, preferred_element_type=F32) * scale
        )
        value_grad = jnp.einsum(
            "hqn,hqd->nd", probs.astype(BF16), grad_rows, preferred_element_type=F32
        )
        stacked = jnp.concatenate([key_grad, value_grad], axis=1).astype(BF16)
        owned = exchange(stacked.reshape(planes, queries, 2 * HD), ZY).astype(F32).sum(axis=0)
        query_pre = rotate(query_grad, cosine, -sine).astype(BF16).reshape(queries, wide)
        key_pre = rotate(owned[:, None, :HD], cosine, -sine)[:, 0].astype(BF16)
        pre = jnp.concatenate([query_pre, key_pre, owned[:, HD:].astype(BF16)], axis=1)

    with jax.named_scope("input_grad"):
        partial = dot(pre, weight_in, ((1,), (1,))).astype(BF16)
        scaled_one = exchange(partial.reshape(4, mine, width), X4).astype(F32).sum(axis=0)
        gain_one_sum = jnp.sum(scaled_one * first_unit, axis=0)
        input_grad = middle_grad + first_factor * (
            scaled_one - first_unit * jnp.mean(scaled_one * first_unit, axis=1, keepdims=True)
        )
        input_grad = spread(input_grad.astype(BF16), xl, core)

    with jax.named_scope("head_grads"):
        in_weight_grad = dot(unit_all, pre, ((0,), (0,)))

        def owned_heads(grad):
            pair = grad.reshape(planes, 2, rows, grad.shape[-1])
            here_half = jnp.where(core == 0, pair[:, 0], pair[:, 1])
            there_half = jnp.where(core == 0, pair[:, 1], pair[:, 0])
            half = (here_half + flip(there_half.astype(BF16), "c").astype(F32)).astype(BF16)
            summed = exchange(half, ZY).astype(F32).sum(axis=0)
            return jnp.where(core == xh, summed, swap(summed.astype(BF16)).astype(F32))

        in_owned = owned_heads(in_weight_grad)
        out_owned = owned_heads(out_weight_grad)

    with jax.named_scope("ffn_grads"):
        owned_pair = hidden_owned.reshape(2, rows, 3 * part)
        kept = jnp.where(xh == 0, owned_pair[0], owned_pair[1])
        sent = flip(jnp.where(xh == 0, owned_pair[1], owned_pair[0]), "xh")
        low = pick(True, xh, kept, sent).reshape(rows, 3, part).astype(F32)
        high = pick(False, xh, kept, sent).reshape(rows, 3, part).astype(F32)
        hidden_full = [
            jnp.concatenate([low[:, i], high[:, i, spare:]], axis=1) for i in range(3)
        ]

    with jax.named_scope("gain_grads"):
        sums = jnp.stack([gain_one_sum, gain_two_sum]).reshape(2, planes * 2, 1, rows)
        sums = jnp.broadcast_to(sums.transpose(1, 2, 0, 3), (planes * 2, 4, 2, rows))
        sums = exchange(sums.reshape(planes * 8, 2, rows), AXES).sum(axis=0)

    return (
        result,
        input_grad,
        sums[0] / gain_one[:, 0],
        gain_one * in_owned[:, :wide],
        gain_one * in_owned[:, wide : wide + HD],
        gain_one * in_owned[:, wide + HD :],
        out_owned.T,
        sums[1] / gain_two[:, 0],
        gain_two * hidden_full[0],
        gain_two * hidden_full[1],
        hidden_full[2].T,
    )


def solution(mesh):
    split = Mesh(mesh.devices.reshape(4, 4, 2, 2, 2), AXES)
    token = P(None, DP, None)
    by_row = P(DP, MP)
    by_column = P(MP, DP)
    in_specs = (
        token, P(), P(), P(DP), by_row, by_row, by_row, by_column,
        P(DP), by_row, by_row, by_column, token,
    )
    out_specs = (
        token, token, P(DP), by_row, by_row, by_row, by_column,
        P(DP), by_row, by_row, by_column,
    )
    return jax.shard_map(
        on_device, mesh=split, in_specs=in_specs, out_specs=out_specs, check_vma=False
    )
```

time: 1750 us -> 533 us (0.30)
  waiting for transfers between devices: 1350 us -> 192 us
  matrix products: 163 us -> 90.6 us
  starting transfers between devices: 47.8 us -> 103 us
  blocking collectives: 23.6 us -> 0 us
    reduce_scatter x17 -> x1, waiting for transfers between devices: 615 us -> 0.02 us  [on_device(): lax.psum_scatter(hidden_weight_grad, ZY, scatter_dimension=0, tiled=True)]
    all_gather x4 -> x1, waiting for transfers between devices: 358 us -> 0.02 us  [on_device(): hidden_weight = lax.all_gather(pair_rows, ZY, axis=0, tiled=True)]
    unnamed x25 -> x2, waiting for transfers between devices: 288 us -> 0.03 us
    all_to_all x8 -> x13, waiting for transfers between devices: 93.2 us -> 169 us  [exchange(): return lax.all_to_all(value, axes, split_axis=0, concat_axis=0, tiled=True)]
    dot_general x54 -> x21, matrix products: 163 us -> 90.6 us  [the longest x15 48.3 us: dot(): return lax.dot_general(a, b, (dims, ((), ())), preferred_element_type=F32)]
    ppermute x0 -> x19, starting transfers between devices: none -> 41.9 us  [the longest x16 24.5 us: flip(): return lax.ppermute(value, axis, [(0, 1), (1, 0)])]
    ppermute x0 -> x19, waiting for transfers between devices: none -> 23.7 us  [the longest x16 19.4 us: flip(): return lax.ppermute(value, axis, [(0, 1), (1, 0)])]
    unnamed x3 -> x0, blocking collectives: 23.6 us -> none
  transfers between devices with their start and end apart: 31 -> 34, of which waited for: 27 -> 17; matrix products, arithmetic and copies ran while one was open for 12% -> 31% of each run, Pallas kernels for 0% -> 0%
where the time goes in v1:
time: 533 us; the launch traced here: 526 us
  waiting for transfers between devices  192 us (36%)
  starting transfers between devices  103 us (19%)
  matrix products  90.6 us (17%)
  other arithmetic  83 us (16%)
  local copies, waits for them, and re-layouts  40.5 us (8%)
  between operations  15.9 us (3%)
    all_to_all x13, waiting for transfers between devices, exchange(): return lax.all_to_all(value, axes, split_axis=0, concat_axis=0, tiled=True)  169 us
    all_to_all x13, starting transfers between devices, exchange(): return lax.all_to_all(value, axes, split_axis=0, concat_axis=0, tiled=True)  61.4 us
    dot_general x15, matrix products, dot(): return lax.dot_general(a, b, (dims, ((), ())), preferred_element_type=F32)  48.3 us
    ppermute x16, starting transfers between devices, flip(): return lax.ppermute(value, axis, [(0, 1), (1, 0)])  24.5 us
    unnamed x144, local copies, waits for them, and re-layouts  22 us
    ppermute x16, waiting for transfers between devices, flip(): return lax.ppermute(value, axis, [(0, 1), (1, 0)])  19.4 us
    ppermute x3, starting transfers between devices, swap(): return lax.ppermute(value, ('xh', 'c'), [(1, 2), (2, 1)])  17.5 us
    dot_general x1, matrix products, on_device(): jnp.einsum('hqd,nd->hqn', grad_rows, values, preferred_element_type=F32)  12.6 us
  transfers between devices with their start and end apart: 34, of which 17 were waited for; matrix products, arithmetic and copies ran while one was open for 31% of the time, Pallas kernels for 0%

profile of v1, /device:TPU:1, one launch (start us, length us, event | category | flops | bytes accessed | tf_op | source)
XLA Modules:
  0.0 525.7 jit_solution(15476258503918689329)
XLA Ops:
  10.3 3.7 collective-permute-start.5
  14.0 6.2 %collective-permute-done.5 = bf16[64,2304]{1,0:T(8,128)(2,1)S(1)} collective-permute-done((bf16[64,2304]{1,0:T(8,128)(2,1)S(1)}, bf16[64,2304]{1,0:T(8,128)(2,1)S(1)}, u32[]{:S(2)}, u32[]{:S(2)}) %collective-permute-start.5) | collective-permute-done | bytes 294944 | tf_op jit(solution)/shard_map/ffn_weights/ppermute | solution.py:32
  21.4 6.6 %collective-permute-start.1 = (bf16[64,1280]{1,0:T(8,128)(2,1)S(1)}, bf16[64,1280]{1,0:T(8,128)(2,1)S(1)}, u32[]{:S(2)}, u32[]{:S(2)}) collective-permute-start(bf16[64,1280]{1,0:T(8,128)(2,1)S(1)} %pad_maximum_fusion.15), channel_id=1, source_target_pairs={{1,4},{4,1},{3,6},{6,3},{9,12},{12,9},{11,14},{14,11},{17,20},{20,... | collective-permute-start | bytes 491528 | tf_op jit(solution)/shard_map/attn_weights/ppermute | solution.py:36
  28.0 3.0 collective-permute-done.1
  32.4 7.8 %all-to-all-start = ((bf16[16,64,768]{2,1,0:T(8,128)(2,1)}), bf16[16,64,768]{2,1,0:T(8,128)(2,1)S(1)}, u32[]{:S(2)}, u32[]{:S(2)}) async-start(bf16[16,64,768]{2,1,0:T(8,128)(2,1)} %broadcast_in_dim.121), calls=%async_computation | async-start | bytes 3145728 | tf_op jit(solution)/shard_map/attn_weights/all_to_all | solution.py:24
  40.4 26.2 %all-to-all-done = bf16[16,64,768]{2,1,0:T(8,128)(2,1)S(1)} async-done(((bf16[16,64,768]{2,1,0:T(8,128)(2,1)}), bf16[16,64,768]{2,1,0:T(8,128)(2,1)S(1)}, u32[]{:S(2)}, u32[]{:S(2)}) %all-to-all-start) | async-done | bytes 1572896 | tf_op jit(solution)/shard_map/attn_weights/all_to_all | solution.py:24
  68.7 4.3 all-to-all-start.2
  74.8 26.8 %all-to-all-done.2 = bf16[16,64,512]{2,1,0:T(8,128)(2,1)} async-done(((bf16[16,64,512]{2,1,0:T(8,128)(2,1)}), bf16[16,64,512]{2,1,0:T(8,128)(2,1)}, u32[]{:S(2)}, u32[]{:S(2)}) %all-to-all-start.2) | async-done | bytes 1048608 | tf_op jit(solution)/shard_map/attn_weights/all_to_all | solution.py:24
  109.7 4.6 all-to-all-start.1
  121.1 33.3 %all-to-all-done.1 = bf16[16,256,256]{2,1,0:T(8,128)(2,1)} async-done(((bf16[16,256,256]{2,1,0:T(8,128)(2,1)}), bf16[16,256,256]{2,1,0:T(8,128)(2,1)}, u32[]{:S(2)}, u32[]{:S(2)}) %all-to-all-start.1) | async-done | bytes 2097184 | tf_op jit(solution)/shard_map/kv_gather/all_to_all | solution.py:24
  154.4 5.1 select_reduce_fusion
  159.5 5.1 fusion.1
  165.6 7.0 %fusion.50 = (bf16[256,4,128]{0,2,1:T(8,128)(2,1)S(1)}, f32[4,256,128]{1,2,0:T(8,128)}) fusion(f32[256,4]{0,1:T(4,128)S(1)} %bitcast.266, bf16[4096,256]{1,0:T(8,128)(2,1)} %bitcast.13, f32[4,256,4096]{2,1,0:T(8,128)S(1)} %get-tuple-element.83, f32[4,256]{1,0:T(4,128)S(1)} %get-tuple-element.82, pred[256,4096]{1,0:T(8,128)(4,1)S(1)} %copy-done.4), kind=kOutput, calls=%fused_computation.104 | convolution fusion | flops 1094975488 | bytes 19668992 | tf_op jit(solution)/shard_map/attend/hqn,nd->hqd/dot_general | solution.py:215
  174.3 3.9 all-to-all-start.3
  179.0 13.6 %all-to-all-done.3 = bf16[4,64,2048]{2,1,0:T(8,128)(2,1)S(1)} async-done(((bf16[4,64,2048]{2,1,0:T(8,128)(2,1)}), bf16[4,64,2048]{2,1,0:T(8,128)(2,1)S(1)}, u32[]{:S(2)}, u32[]{:S(2)}) %all-to-all-start.3) | async-done | bytes 1048608 | tf_op jit(solution)/shard_map/branch/all_to_all | solution.py:24
  195.7 4.2 all-to-all-start.4
  201.1 2.9 collective-permute-start.9
  204.1 9.4 %all-to-all-done.4 = bf16[4,64,2048]{2,1,0:T(8,128)(2,1)} async-done(((bf16[4,64,2048]{2,1,0:T(8,128)(2,1)}), bf16[4,64,2048]{2,1,0:T(8,128)(2,1)}, u32[]{:S(2)}, u32[]{:S(2)}) %all-to-all-start.4) | async-done | bytes 1048608 | tf_op jit(solution)/shard_map/branch/all_to_all | solution.py:24
  213.4 5.1 collective-permute-start.4
  220.1 4.6 collective-permute-done.9
  227.8 2.7 collective-permute-start.10
  230.5 4.5 fusion.29
  235.8 3.4 fusion.25
  239.2 3.5 multiply_convert_fusion.2
  242.7 3.9 convolution_convert_fusion
  246.6 3.4 convolution_convert_fusion.1
  250.0 3.4 convolution_convert_fusion.2
  253.4 4.9 pad_maximum_fusion
  258.3 12.3 %copy.344 = bf16[2048,2304]{1,0:T(8,128)(2,1)} copy(bf16[2048,2304]{0,1:T(8,128)(2,1)} %pad_maximum_fusion) | data formatting | bytes 18874368
  270.7 4.0 fusion.27
  274.7 3.8 convolution_add_fusion
  278.8 3.7 fusion.22
  285.5 4.2 all-to-all-start.6
  289.8 3.4 fusion.34
  293.2 11.8 %all-to-all-done.6 = bf16[4,64,2048]{2,1,0:T(8,128)(2,1)} async-done(((bf16[4,64,2048]{2,1,0:T(8,128)(2,1)}), bf16[4,64,2048]{2,1,0:T(8,128)(2,1)}, u32[]{:S(2)}, u32[]{:S(2)}) %all-to-all-start.6) | async-done | bytes 1048608 | tf_op jit(solution)/shard_map/ffn_back/all_to_all | solution.py:24
  304.9 4.2 all-to-all-start.5
  311.4 12.0 %all-to-all-done.5 = bf16[4,64,2048]{2,1,0:T(8,128)(2,1)} async-done(((bf16[4,64,2048]{2,1,0:T(8,128)(2,1)}), bf16[4,64,2048]{2,1,0:T(8,128)(2,1)}, u32[]{:S(2)}, u32[]{:S(2)}) %all-to-all-start.5) | async-done | bytes 1048608 | tf_op jit(solution)/shard_map/result/all_to_all | solution.py:24
  328.3 4.4 all-to-all-start.7
  337.0 8.7 %all-to-all-done.7 = bf16[4,64,2048]{2,1,0:T(8,128)(2,1)} async-done(((bf16[4,64,2048]{2,1,0:T(8,128)(2,1)}), bf16[4,64,2048]{2,1,0:T(8,128)(2,1)}, u32[]{:S(2)}, u32[]{:S(2)}) %all-to-all-start.7) | async-done | bytes 1048608 | tf_op jit(solution)/shard_map/ffn_back/all_to_all | solution.py:24
  345.7 2.7 convolution_convert_fusion.5
  350.7 12.6 %multiply_convert_fusion = bf16[4,256,4096]{2,1,0:T(8,128)(2,1)} fusion(f32[4,256,4096]{2,1,0:T(8,128)} %copy-done.1, bf16[4,256,128]{1,2,0:T(8,128)(2,1)S(1)} %bitcast.243, f32[4,256]{1,0:T(4,128)S(1)} %multiply_reduce_fusion, f32[4,256]{1,0:T(4,128)} %log_add_fusion, pred[256,4096]{1,0:T(8,128)(4,1)} %compare_and_fusion, bf16[4096,256]{1,0:T(8,128)(2,1)} %bitcast.13), kind=kOutput, calls=%fused_computation | convolution fusion | flops 1098907648 | bytes 27533312 | tf_op jit(solution)/shard_map/attend_back/hqd,nd->hqn/dot_general | solution.py:276
  363.3 6.0 %fusion.13 = bf16[4096,128]{1,0:T(8,128)(2,1)S(1)} fusion(bf16[4,256,4096]{2,1,0:T(8,128)(2,1)} %multiply_convert_fusion, bf16[256,4,64]{2,0,1:T(8,128)(2,1)S(1)} %copy-done.25, bf16[256,4,64]{2,0,1:T(8,128)(2,1)S(1)} %copy-done.23), kind=kOutput, calls=%fused_computation.15 | convolution fusion | flops 1075314688 | bytes 9699328 | tf_op jit(solution)/shard_map/attend_back/hqn,hqd->nd/dot_general | solution.py:280
  369.4 5.5 %fusion.14 = bf16[4096,128]{1,0:T(8,128)(2,1)S(1)} fusion(bf16[4,256,128]{1,2,0:T(8,128)(2,1)S(1)} %bitcast.244, f32[4,256,4096]{2,1,0:T(8,128)S(1)} %bitcast.231, f32[4,256]{1,0:T(4,128)S(1)} %copy-done.47, pred[256,4096]{1,0:T(8,128)(4,1)S(1)} %copy-done.5), kind=kOutput, calls=%fused_computation.16 | convolution fusion | flops 1091043328 | bytes 19140608 | tf_op jit(solution)/shard_map/attend_back/hqn,hqd->nd/dot_general | solution.py:282
  376.6 3.9 all-to-all-start.8
  380.6 2.3 copy.321
  382.8 2.0 fusion.101
  388.0 3.0 collective-permute-start.16
  391.8 6.1 %fusion.40 = f32[256,4,128]{2,0,1:T(8,128)S(1)} fusion(bf16[4,256,4096]{2,1,0:T(8,128)(2,1)} %multiply_convert_fusion, bf16[4096,256]{1,0:T(8,128)(2,1)} %bitcast.13), kind=kOutput, calls=%fused_computation.76 | convolution fusion | flops 1073872896 | bytes 9961472 | tf_op jit(solution)/shard_map/attend_back/hqn,nd->qhd/dot_general | solution.py:278
  400.8 4.1 fusion.37
  405.7 7.4 %all-to-all-start.12 = ((bf16[16,64,512]{2,1,0:T(8,128)(2,1)}), bf16[16,64,512]{2,1,0:T(8,128)(2,1)}, u32[]{:S(2)}, u32[]{:S(2)}) async-start(bf16[16,64,512]{2,1,0:T(8,128)(2,1)} %fusion.37), calls=%async_computation.12 | async-start | bytes 2097152 | tf_op jit(solution)/shard_map/head_grads/all_to_all | solution.py:24
  414.1 5.2 fusion.55
  421.3 6.8 %all-to-all-done.12 = bf16[16,64,512]{2,1,0:T(8,128)(2,1)} async-done(((bf16[16,64,512]{2,1,0:T(8,128)(2,1)}), bf16[16,64,512]{2,1,0:T(8,128)(2,1)}, u32[]{:S(2)}, u32[]{:S(2)}) %all-to-all-start.12) | async-done | bytes 1048608 | tf_op jit(solution)/shard_map/head_grads/all_to_all | solution.py:24
  428.1 3.5 all-to-all-start.9
  431.7 4.3 fusion.38
  436.0 3.6 collective-permute-start.14
  439.6 2.2 select_bitcast_fusion.7
  443.8 5.1 collective-permute-start.17
  452.1 4.8 all-to-all-start.10
  456.9 5.1 fusion.19
  462.0 4.4 all-to-all-done.10
  467.0 4.0 all-to-all-start.11
  479.6 14.9 %all-to-all-done.11 = bf16[16,64,768]{2,1,0:T(8,128)(2,1)S(1)} async-done(((bf16[16,64,768]{2,1,0:T(8,128)(2,1)}), bf16[16,64,768]{2,1,0:T(8,128)(2,1)S(1)}, u32[]{:S(2)}, u32[]{:S(2)}) %all-to-all-start.11) | async-done | bytes 1572896 | tf_op jit(solution)/shard_map/head_grads/all_to_all | solution.py:24
  494.8 5.8 %collective-permute-start.15 = (bf16[64,768]{1,0:T(8,128)(2,1)S(1)}, bf16[64,768]{1,0:T(8,128)(2,1)S(1)}, u32[]{:S(2)}, u32[]{:S(2)}) collective-permute-start(bf16[64,768]{1,0:T(8,128)(2,1)S(1)} %convert_element_type.286), channel_id=1, source_target_pairs={{1,4},{4,1},{3,6},{6,3},{9,12},{12,9},{11,14},{14,11},{17,20},{20,... | collective-permute-start | bytes 294920 | tf_op jit(solution)/shard_map/head_grads/ppermute | solution.py:36
  505.6 8.6 %collective-permute-done.18 = bf16[64,2304]{1,0:T(8,128)(2,1)S(1)} collective-permute-done((bf16[64,2304]{1,0:T(8,128)(2,1)S(1)}, bf16[64,2304]{1,0:T(8,128)(2,1)S(1)}, u32[]{:S(2)}, u32[]{:S(2)}) %collective-permute-start.18) | collective-permute-done | bytes 294944 | tf_op jit(solution)/shard_map/ffn_grads/ppermute | solution.py:32
  (301 shorter events, 90.2 us)
Async XLA Ops:
  7.2 223.3 %all-gather.2.cloned.1.call-start = ((), (), s32[]{:S(2)}) async-start(), calls=%async_computation.14 | async-start | bytes 10027008 | tf_op jit(solution)/shard_map/ffn_weights/all_gather | solution.py:164
  9.0 12.1 %copy-start.54 = (bf16[64]{0:T(256)(128)(2,1)S(1)}, bf16[64]{0:T(256)(128)(2,1)}, u32[]{:S(2)}) copy-start(bf16[64]{0:T(256)(128)(2,1)} %param.16) | copy-start | bytes 388
  9.1 12.2 %copy-start.36 = (bf16[64,128]{1,0:T(8,128)(2,1)S(1)}, bf16[64,128]{1,0:T(8,128)(2,1)}, u32[]{:S(2)}) copy-start(bf16[64,128]{1,0:T(8,128)(2,1)} %param.18) | copy-start | bytes 49156
  9.1 12.1 %copy-start.37 = (bf16[64,128]{1,0:T(8,128)(2,1)S(1)}, bf16[64,128]{1,0:T(8,128)(2,1)}, u32[]{:S(2)}) copy-start(bf16[64,128]{1,0:T(8,128)(2,1)} %param.19) | copy-start | bytes 49156
  9.1 12.2 %copy-start.29 = (bf16[64,512]{1,0:T(8,128)(2,1)S(1)}, bf16[64,512]{1,0:T(8,128)(2,1)}, u32[]{:S(2)}) copy-start(bf16[64,512]{1,0:T(8,128)(2,1)} %param.17) | copy-start | bytes 196612
  9.1 12.3 %copy-start.26 = (bf16[512,64]{0,1:T(8,128)(2,1)S(1)}, bf16[512,64]{0,1:T(8,128)(2,1)}, u32[]{:S(2)}) copy-start(bf16[512,64]{0,1:T(8,128)(2,1)} %param.20) | copy-start | bytes 196612
  10.3 9.9 %collective-permute-start.5 = (bf16[64,2304]{1,0:T(8,128)(2,1)S(1)}, bf16[64,2304]{1,0:T(8,128)(2,1)S(1)}, u32[]{:S(2)}, u32[]{:S(2)}) collective-permute-start(bf16[64,2304]{1,0:T(8,128)(2,1)S(1)} %bitcast.258), channel_id=1, source_target_pairs={{0,4},{4,0},{1,5},{5,1},{2,6},{6,2},{3,7},{7,3},{8,12},{12,8},{9,1... | collective-permute-start | bytes 884744 | tf_op jit(solution)/shard_map/ffn_weights/ppermute | solution.py:32
  21.2 19.0 %copy-start.6 = (bf16[2,128,2048]{2,1,0:T(8,128)(2,1)S(1)}, bf16[2,128,2048]{2,1,0:T(8,128)(2,1)}, u32[]{:S(2)}) copy-start(bf16[2,128,2048]{2,1,0:T(8,128)(2,1)} %param.13) | copy-start | bytes 3145732
  21.2 11.2 %copy-start.43 = (f32[64]{0:T(128)}, f32[64]{0:T(128)S(1)}, u32[]{:S(2)}) copy-start(f32[64]{0:T(128)S(1)} %convert_element_type.235) | copy-start | bytes 772
  21.4 9.6 %collective-permute-start.1 = (bf16[64,1280]{1,0:T(8,128)(2,1)S(1)}, bf16[64,1280]{1,0:T(8,128)(2,1)S(1)}, u32[]{:S(2)}, u32[]{:S(2)}) collective-permute-start(bf16[64,1280]{1,0:T(8,128)(2,1)S(1)} %pad_maximum_fusion.15), channel_id=1, source_target_pairs={{1,4},{4,1},{3,6},{6,3},{9,12},{12,9},{11,14},{14,11},{17,20},{20,... | collective-permute-start | bytes 491528 | tf_op jit(solution)/shard_map/attn_weights/ppermute | solution.py:36
  31.1 9.3 %copy-start.32 = (s32[2,4096]{1,0:T(2,128)S(1)}, s32[2,4096]{1,0:T(2,128)}, u32[]{:S(2)}) copy-start(s32[2,4096]{1,0:T(2,128)} %param.14) | copy-start | bytes 98308
  31.1 35.6 %copy-start.52 = (s32[2,2]{1,0:T(2,128)S(1)}, s32[2,2]{1,0:T(2,128)}, u32[]{:S(2)}) copy-start(s32[2,2]{1,0:T(2,128)} %param.15) | copy-start | bytes 52
  32.4 34.3 %all-to-all-start = ((bf16[16,64,768]{2,1,0:T(8,128)(2,1)}), bf16[16,64,768]{2,1,0:T(8,128)(2,1)S(1)}, u32[]{:S(2)}, u32[]{:S(2)}) async-start(bf16[16,64,768]{2,1,0:T(8,128)(2,1)} %broadcast_in_dim.121), calls=%async_computation | async-start | bytes 3145728 | tf_op jit(solution)/shard_map/attn_weights/all_to_all | solution.py:24
  40.2 32.9 %collective-permute-start = (bf16[128,2048]{1,0:T(8,128)(2,1)S(1)}, bf16[128,2048]{1,0:T(8,128)(2,1)}, u32[]{:S(2)}, u32[]{:S(2)}) collective-permute-start(bf16[128,2048]{1,0:T(8,128)(2,1)S(1)} %dynamic-slice_bitcast_fusion.1), channel_id=1, source_target_pairs={{0,4},{4,0},{1,5},{5,1},{2,6},{6,2},{3,7},{7,3},{8,12},{12,8},{9,1... | collective-permute-start | bytes 1572872 | tf_op jit(solution)/shard_map/first_norm/ppermute | solution.py:32
  66.6 36.3 %collective-permute-start.2 = (bf16[16,64,768]{2,1,0:T(8,128)(2,1)S(1)}, bf16[16,64,768]{2,1,0:T(8,128)(2,1)}, u32[]{:S(2)}, u32[]{:S(2)}) collective-permute-start(bf16[16,64,768]{2,1,0:T(8,128)(2,1)S(1)} %all-to-all-done), channel_id=1, source_target_pairs={{0,1},{1,0},{2,3},{3,2},{4,5},{5,4},{6,7},{7,6},{8,9},{9,8},{10,11... | collective-permute-start | bytes 4718600 | tf_op jit(solution)/shard_map/attn_weights/ppermute | solution.py:32
  68.7 32.8 %all-to-all-start.2 = ((bf16[16,64,512]{2,1,0:T(8,128)(2,1)}), bf16[16,64,512]{2,1,0:T(8,128)(2,1)}, u32[]{:S(2)}, u32[]{:S(2)}) async-start(bf16[16,64,512]{2,1,0:T(8,128)(2,1)} %broadcast_in_dim.125), calls=%async_computation.2 | async-start | bytes 2097152 | tf_op jit(solution)/shard_map/attn_weights/all_to_all | solution.py:24
  73.1 41.2 %copy-start.45 = (f32[64]{0:T(128)}, f32[64]{0:T(128)S(1)}, u32[]{:S(2)}) copy-start(f32[64]{0:T(128)S(1)} %multiply_exponential_fusion) | copy-start | bytes 772
  73.1 41.2 %copy-start.34 = (f32[256]{0:T(256)}, f32[256]{0:T(256)S(1)}, u32[]{:S(2)}) copy-start(f32[256]{0:T(256)S(1)} %dynamic-slice_convert_fusion.1) | copy-start | bytes 3076
  74.4 30.5 %copy-start.2 = (bf16[128,2048]{1,0:T(8,128)(2,1)}, bf16[128,2048]{1,0:T(8,128)(2,1)S(1)}, u32[]{:S(2)}) copy-start(bf16[128,2048]{1,0:T(8,128)(2,1)S(1)} %get-tuple-element.35) | copy-start | bytes 1572868
  74.4 30.5 %copy-start.3 = (bf16[128,2048]{1,0:T(8,128)(2,1)}, bf16[128,2048]{1,0:T(8,128)(2,1)S(1)}, u32[]{:S(2)}) copy-start(bf16[128,2048]{1,0:T(8,128)(2,1)S(1)} %get-tuple-element.36) | copy-start | bytes 1572868
  74.7 30.2 %copy-start.40 = (f32[256]{0:T(256)}, f32[256]{0:T(256)S(1)}, u32[]{:S(2)}) copy-start(f32[256]{0:T(256)S(1)} %add_rsqrt_fusion) | copy-start | bytes 3076
  101.5 16.0 %collective-permute-start.3 = (bf16[16,64,512]{2,1,0:T(8,128)(2,1)}, bf16[16,64,512]{2,1,0:T(8,128)(2,1)}, u32[]{:S(2)}, u32[]{:S(2)}) collective-permute-start(bf16[16,64,512]{2,1,0:T(8,128)(2,1)} %all-to-all-done.2), channel_id=1, source_target_pairs={{0,1},{1,0},{2,3},{3,2},{4,5},{5,4},{6,7},{7,6},{8,9},{9,8},{10,11... | collective-permute-start | bytes 3145736 | tf_op jit(solution)/shard_map/attn_weights/ppermute | solution.py:32
  109.7 44.7 %all-to-all-start.1 = ((bf16[16,256,256]{2,1,0:T(8,128)(2,1)}), bf16[16,256,256]{2,1,0:T(8,128)(2,1)}, u32[]{:S(2)}, u32[]{:S(2)}) async-start(bf16[16,256,256]{2,1,0:T(8,128)(2,1)} %broadcast_in_dim.122), calls=%async_computation.1 | async-start | bytes 4194304 | tf_op jit(solution)/shard_map/kv_gather/all_to_all | solution.py:24
  121.1 38.4 %copy-start.22 = (bf16[256,4,64]{2,0,1:T(8,128)(2,1)}, bf16[256,4,64]{2,0,1:T(8,128)(2,1)S(1)}, u32[]{:S(2)}) copy-start(bf16[256,4,64]{2,0,1:T(8,128)(2,1)S(1)} %get-tuple-element.26) | copy-start | bytes 393220
  121.1 38.4 %copy-start.24 = (bf16[256,4,64]{2,0,1:T(8,128)(2,1)}, bf16[256,4,64]{2,0,1:T(8,128)(2,1)S(1)}, u32[]{:S(2)}) copy-start(bf16[256,4,64]{2,0,1:T(8,128)(2,1)S(1)} %get-tuple-element.27) | copy-start | bytes 393220
  172.6 20.2 %copy-start.18 = (bf16[256,4,128]{0,2,1:T(8,128)(2,1)}, bf16[256,4,128]{0,2,1:T(8,128)(2,1)S(1)}, u32[]{:S(2)}) copy-start(bf16[256,4,128]{0,2,1:T(8,128)(2,1)S(1)} %get-tuple-element.84) | copy-start | bytes 786436
  174.3 18.3 %all-to-all-start.3 = ((bf16[4,64,2048]{2,1,0:T(8,128)(2,1)}), bf16[4,64,2048]{2,1,0:T(8,128)(2,1)S(1)}, u32[]{:S(2)}, u32[]{:S(2)}) async-start(bf16[4,64,2048]{2,1,0:T(8,128)(2,1)} %bitcast.234), calls=%async_computation.3 | async-start | bytes 2097152 | tf_op jit(solution)/shard_map/branch/all_to_all | solution.py:24
  194.5 130.4 %copy-start.42 = (f32[64]{0:T(128)}, f32[64]{0:T(128)S(1)}, u32[]{:S(2)}) copy-start(f32[64]{0:T(128)S(1)} %add_rsqrt_fusion.2) | copy-start | bytes 772
  195.7 17.7 %all-to-all-start.4 = ((bf16[4,64,2048]{2,1,0:T(8,128)(2,1)}), bf16[4,64,2048]{2,1,0:T(8,128)(2,1)}, u32[]{:S(2)}, u32[]{:S(2)}) async-start(bf16[4,64,2048]{2,1,0:T(8,128)(2,1)} %broadcast_in_dim.126), calls=%async_computation.4 | async-start | bytes 2097152 | tf_op jit(solution)/shard_map/branch/all_to_all | solution.py:24
  200.0 303.0 %reduce-scatter.4.cloned.1.call-start = ((), (), s32[]{:S(2)}) async-start(), calls=%async_computation.15 | async-start | bytes 10027008 | tf_op jit(solution)/shard_map/ffn_back/reduce_scatter | solution.py:258
  201.1 23.6 %collective-permute-start.9 = (bf16[128,2048]{1,0:T(8,128)(2,1)S(1)}, bf16[128,2048]{1,0:T(8,128)(2,1)}, u32[]{:S(2)}, u32[]{:S(2)}) collective-permute-start(bf16[128,2048]{1,0:T(8,128)(2,1)S(1)} %dynamic-slice_bitcast_fusion), channel_id=1, source_target_pairs={{0,4},{4,0},{1,5},{5,1},{2,6},{6,2},{3,7},{7,3},{8,12},{12,8},{9,1... | collective-permute-start | bytes 1572872 | tf_op jit(solution)/shard_map/cotangent/ppermute | solution.py:32
  213.4 17.0 %collective-permute-start.4 = (bf16[256,2048]{1,0:T(8,128)(2,1)}, bf16[256,2048]{1,0:T(8,128)(2,1)}, u32[]{:S(2)}, u32[]{:S(2)}) collective-permute-start(bf16[256,2048]{1,0:T(8,128)(2,1)} %bitcast.24), channel_id=1, source_target_pairs={{0,1},{1,0},{2,3},{3,2},{4,5},{5,4},{6,7},{7,6},{8,9},{9,8},{10,11... | collective-permute-start | bytes 3145736 | tf_op jit(solution)/shard_map/branch/ppermute | solution.py:32
  227.8 11.3 %collective-permute-start.10 = (bf16[256,2048]{1,0:T(8,128)(2,1)}, bf16[256,2048]{1,0:T(8,128)(2,1)}, u32[]{:S(2)}, u32[]{:S(2)}) collective-permute-start(bf16[256,2048]{1,0:T(8,128)(2,1)} %pad_maximum_fusion.7), channel_id=1, source_target_pairs={{0,1},{1,0},{2,3},{3,2},{4,5},{5,4},{6,7},{7,6},{8,9},{9,8},{10,11... | collective-permute-start | bytes 3145736 | tf_op jit(solution)/shard_map/cotangent/ppermute | solution.py:32
  278.7 5.6 %collective-permute-start.11 = (bf16[256,2048]{1,0:T(8,128)(2,1)S(1)}, bf16[256,2048]{1,0:T(8,128)(2,1)S(1)}, u32[]{:S(2)}, u32[]{:S(2)}) collective-permute-start(bf16[256,2048]{1,0:T(8,128)(2,1)S(1)} %slice.287), channel_id=1, source_target_pairs={{0,1},{1,0},{2,3},{3,2},{4,5},{5,4},{6,7},{7,6},{8,9},{9,8},{10,11... | collective-permute-start | bytes 3145736 | tf_op jit(solution)/shard_map/ffn_back/ppermute | solution.py:32
  283.8 6.0 %collective-permute-start.6 = (bf16[256,2048]{1,0:T(8,128)(2,1)}, bf16[256,2048]{1,0:T(8,128)(2,1)}, u32[]{:S(2)}, u32[]{:S(2)}) collective-permute-start(bf16[256,2048]{1,0:T(8,128)(2,1)} %slice.288), channel_id=1, source_target_pairs={{0,1},{1,0},{2,3},{3,2},{4,5},{5,4},{6,7},{7,6},{8,9},{9,8},{10,11... | collective-permute-start | bytes 3145736 | tf_op jit(solution)/shard_map/result/ppermute | solution.py:32
  285.5 19.4 %all-to-all-start.6 = ((bf16[4,64,2048]{2,1,0:T(8,128)(2,1)}), bf16[4,64,2048]{2,1,0:T(8,128)(2,1)}, u32[]{:S(2)}, u32[]{:S(2)}) async-start(bf16[4,64,2048]{2,1,0:T(8,128)(2,1)} %bitcast.236), calls=%async_computation.6 | async-start | bytes 2097152 | tf_op jit(solution)/shard_map/ffn_back/all_to_all | solution.py:24
  304.9 18.5 %all-to-all-start.5 = ((bf16[4,64,2048]{2,1,0:T(8,128)(2,1)}), bf16[4,64,2048]{2,1,0:T(8,128)(2,1)}, u32[]{:S(2)}, u32[]{:S(2)}) async-start(bf16[4,64,2048]{2,1,0:T(8,128)(2,1)} %bitcast.235), calls=%async_computation.5 | async-start | bytes 2097152 | tf_op jit(solution)/shard_map/result/all_to_all | solution.py:24
  326.9 8.4 %collective-permute-start.7 = (bf16[64,2048]{1,0:T(8,128)(2,1)}, bf16[64,2048]{1,0:T(8,128)(2,1)}, u32[]{:S(2)}, u32[]{:S(2)}) collective-permute-start(bf16[64,2048]{1,0:T(8,128)(2,1)} %get-tuple-element.52), channel_id=1, source_target_pairs={{0,2},{2,0},{1,3},{3,1},{4,6},{6,4},{5,7},{7,5},{8,10},{10,8},{9,1... | collective-permute-start | bytes 786440 | tf_op jit(solution)/shard_map/result/ppermute | solution.py:32
  328.3 17.4 %all-to-all-start.7 = ((bf16[4,64,2048]{2,1,0:T(8,128)(2,1)}), bf16[4,64,2048]{2,1,0:T(8,128)(2,1)}, u32[]{:S(2)}, u32[]{:S(2)}) async-start(bf16[4,64,2048]{2,1,0:T(8,128)(2,1)} %broadcast_in_dim.129), calls=%async_computation.7 | async-start | bytes 2097152 | tf_op jit(solution)/shard_map/ffn_back/all_to_all | solution.py:24
  350.6 12.7 %copy-start.23 = (bf16[256,4,64]{2,0,1:T(8,128)(2,1)S(1)}, bf16[256,4,64]{2,0,1:T(8,128)(2,1)}, u32[]{:S(2)}) copy-start(bf16[256,4,64]{2,0,1:T(8,128)(2,1)} %copy-done.22) | copy-start | bytes 393220
  350.6 12.7 %copy-start.25 = (bf16[256,4,64]{2,0,1:T(8,128)(2,1)S(1)}, bf16[256,4,64]{2,0,1:T(8,128)(2,1)}, u32[]{:S(2)}) copy-start(bf16[256,4,64]{2,0,1:T(8,128)(2,1)} %copy-done.24) | copy-start | bytes 393220
  350.6 18.7 %slice-start = ((s8[16777216]{0:T(1024)(128)(4,1)}), s8[4194304]{0:T(1024)(128)(4,1)S(1)}, s32[]{:S(2)}) async-start(s8[16777216]{0:T(1024)(128)(4,1)} %bitcast.230), calls=%async_computation.16 | async-start | bytes 8388608
  350.6 18.7 %slice-start.1 = ((s8[16777216]{0:T(1024)(128)(4,1)}), s8[4194304]{0:T(1024)(128)(4,1)S(1)}, s32[]{:S(2)}) async-start(s8[16777216]{0:T(1024)(128)(4,1)} %bitcast.230), calls=%async_computation.17 | async-start | bytes 8388608
  350.7 18.7 %slice-start.2 = ((s8[16777216]{0:T(1024)(128)(4,1)}), s8[4194304]{0:T(1024)(128)(4,1)S(1)}, s32[]{:S(2)}) async-start(s8[16777216]{0:T(1024)(128)(4,1)} %bitcast.230), calls=%async_computation.18 | async-start | bytes 8388608
  376.6 29.1 %all-to-all-start.8 = ((bf16[16,256,256]{2,1,0:T(8,128)(2,1)}), bf16[16,256,256]{2,1,0:T(8,128)(2,1)S(1)}, u32[]{:S(2)}, u32[]{:S(2)}) async-start(bf16[16,256,256]{2,1,0:T(8,128)(2,1)} %pad_maximum_fusion.4), calls=%async_computation.8 | async-start | bytes 4194304 | tf_op jit(solution)/shard_map/attend_back/all_to_all | solution.py:24
  388.0 12.8 %collective-permute-start.16 = (bf16[16,64,512]{2,1,0:T(8,128)(2,1)}, bf16[16,64,512]{2,1,0:T(8,128)(2,1)}, u32[]{:S(2)}, u32[]{:S(2)}) collective-permute-start(bf16[16,64,512]{2,1,0:T(8,128)(2,1)} %fusion.41), channel_id=1, source_target_pairs={{0,1},{1,0},{2,3},{3,2},{4,5},{5,4},{6,7},{7,6},{8,9},{9,8},{10,11... | collective-permute-start | bytes 3145736 | tf_op jit(solution)/shard_map/head_grads/ppermute | solution.py:32
  391.8 47.7 %collective-permute-start.8 = (bf16[128,2048]{1,0:T(8,128)(2,1)}, bf16[128,2048]{1,0:T(8,128)(2,1)}, u32[]{:S(2)}, u32[]{:S(2)}) collective-permute-start(bf16[128,2048]{1,0:T(8,128)(2,1)} %pad_maximum_fusion.11), channel_id=1, source_target_pairs={{0,1},{1,0},{2,3},{3,2},{4,5},{5,4},{6,7},{7,6},{8,9},{9,8},{10,11... | collective-permute-start | bytes 1572872 | tf_op jit(solution)/shard_map/result/ppermute | solution.py:32
  405.0 8.7 %copy-start.46 = (f32[64]{0:T(128)S(1)}, f32[64]{0:T(128)}, u32[]{:S(2)}) copy-start(f32[64]{0:T(128)} %copy-done.45) | copy-start | bytes 772
  405.0 9.1 %copy-start.41 = (f32[256]{0:T(256)S(1)}, f32[256]{0:T(256)}, u32[]{:S(2)}) copy-start(f32[256]{0:T(256)} %copy-done.40) | copy-start | bytes 3076
  405.7 22.4 %all-to-all-start.12 = ((bf16[16,64,512]{2,1,0:T(8,128)(2,1)}), bf16[16,64,512]{2,1,0:T(8,128)(2,1)}, u32[]{:S(2)}, u32[]{:S(2)}) async-start(bf16[16,64,512]{2,1,0:T(8,128)(2,1)} %fusion.37), calls=%async_computation.12 | async-start | bytes 2097152 | tf_op jit(solution)/shard_map/head_grads/all_to_all | solution.py:24
  428.1 20.8 %all-to-all-start.9 = ((bf16[4,64,2048]{2,1,0:T(8,128)(2,1)}), bf16[4,64,2048]{2,1,0:T(8,128)(2,1)S(1)}, u32[]{:S(2)}, u32[]{:S(2)}) async-start(bf16[4,64,2048]{2,1,0:T(8,128)(2,1)} %bitcast.52), calls=%async_computation.9 | async-start | bytes 2097152 | tf_op jit(solution)/shard_map/input_grad/all_to_all | solution.py:24
  436.0 13.1 %copy-start.7 = (bf16[2,128,2048]{2,1,0:T(8,128)(2,1)S(1)}, bf16[2,128,2048]{2,1,0:T(8,128)(2,1)}, u32[]{:S(2)}) copy-start(bf16[2,128,2048]{2,1,0:T(8,128)(2,1)} %param.13) | copy-start | bytes 3145732
  436.0 13.1 %copy-start.51 = (f32[64]{0:T(128)S(1)}, f32[64]{0:T(128)}, u32[]{:S(2)}) copy-start(f32[64]{0:T(128)} %add_rsqrt_fusion.1) | copy-start | bytes 772
  436.0 20.9 %collective-permute-start.14 = (bf16[16,64,768]{2,1,0:T(8,128)(2,1)}, bf16[16,64,768]{2,1,0:T(8,128)(2,1)}, u32[]{:S(2)}, u32[]{:S(2)}) collective-permute-start(bf16[16,64,768]{2,1,0:T(8,128)(2,1)} %fusion.38), channel_id=1, source_target_pairs={{0,1},{1,0},{2,3},{3,2},{4,5},{5,4},{6,7},{7,6},{8,9},{9,8},{10,11... | collective-permute-start | bytes 4718600 | tf_op jit(solution)/shard_map/head_grads/ppermute | solution.py:32
  443.8 30.9 %collective-permute-start.17 = (bf16[64,512]{1,0:T(8,128)(2,1)}, bf16[64,512]{1,0:T(8,128)(2,1)}, u32[]{:S(2)}, u32[]{:S(2)}) collective-permute-start(bf16[64,512]{1,0:T(8,128)(2,1)} %convert_element_type.293), channel_id=1, source_target_pairs={{1,4},{4,1},{3,6},{6,3},{9,12},{12,9},{11,14},{14,11},{17,20},{20,... | collective-permute-start | bytes 196616 | tf_op jit(solution)/shard_map/head_grads/ppermute | solution.py:36
  450.7 20.3 %collective-permute-start.12 = (bf16[64,2048]{1,0:T(8,128)(2,1)S(1)}, bf16[64,2048]{1,0:T(8,128)(2,1)}, u32[]{:S(2)}, u32[]{:S(2)}) collective-permute-start(bf16[64,2048]{1,0:T(8,128)(2,1)S(1)} %fusion.48), channel_id=1, source_target_pairs={{0,2},{2,0},{1,3},{3,1},{4,6},{6,4},{5,7},{7,5},{8,10},{10,8},{9,1... | collective-permute-start | bytes 786440 | tf_op jit(solution)/shard_map/input_grad/ppermute | solution.py:32
  452.1 14.3 %all-to-all-start.10 = ((f32[128,1,128]{2,1,0:T(1,128)}), f32[128,1,128]{2,1,0:T(1,128)S(1)}, u32[]{:S(2)}, u32[]{:S(2)}) async-start(f32[128,1,128]{2,1,0:T(1,128)} %reshape.424), calls=%async_computation.10 | async-start | bytes 131072 | tf_op jit(solution)/shard_map/gain_grads/all_to_all | solution.py:24
  462.0 11.6 %copy-start.13 = (bf16[1,128,2048]{2,1,0:T(8,128)(2,1)S(1)}, bf16[1,128,2048]{2,1,0:T(8,128)(2,1)}, u32[]{:S(2)}) copy-start(bf16[1,128,2048]{2,1,0:T(8,128)(2,1)} %get-tuple-element.33) | copy-start | bytes 1572868
  462.0 11.6 %copy-start.14 = (bf16[1,128,2048]{2,1,0:T(8,128)(2,1)S(1)}, bf16[1,128,2048]{2,1,0:T(8,128)(2,1)}, u32[]{:S(2)}) copy-start(bf16[1,128,2048]{2,1,0:T(8,128)(2,1)} %get-tuple-element.34) | copy-start | bytes 1572868
  467.0 27.6 %all-to-all-start.11 = ((bf16[16,64,768]{2,1,0:T(8,128)(2,1)}), bf16[16,64,768]{2,1,0:T(8,128)(2,1)S(1)}, u32[]{:S(2)}, u32[]{:S(2)}) async-start(bf16[16,64,768]{2,1,0:T(8,128)(2,1)} %fusion.19), calls=%async_computation.11 | async-start | bytes 3145728 | tf_op jit(solution)/shard_map/head_grads/all_to_all | solution.py:24
  472.9 5.5 %collective-permute-start.13 = (bf16[128,2048]{1,0:T(8,128)(2,1)}, bf16[128,2048]{1,0:T(8,128)(2,1)}, u32[]{:S(2)}, u32[]{:S(2)}) collective-permute-start(bf16[128,2048]{1,0:T(8,128)(2,1)} %pad_maximum_fusion.12), channel_id=1, source_target_pairs={{0,1},{1,0},{2,3},{3,2},{4,5},{5,4},{6,7},{7,6},{8,9},{9,8},{10,11... | collective-permute-start | bytes 1572872 | tf_op jit(solution)/shard_map/input_grad/ppermute | solution.py:32
  479.6 24.5 %copy-start.44 = (f32[64]{0:T(128)S(1)}, f32[64]{0:T(128)}, u32[]{:S(2)}) copy-start(f32[64]{0:T(128)} %copy-done.43) | copy-start | bytes 772
  494.8 8.1 %collective-permute-start.15 = (bf16[64,768]{1,0:T(8,128)(2,1)S(1)}, bf16[64,768]{1,0:T(8,128)(2,1)S(1)}, u32[]{:S(2)}, u32[]{:S(2)}) collective-permute-start(bf16[64,768]{1,0:T(8,128)(2,1)S(1)} %convert_element_type.286), channel_id=1, source_target_pairs={{1,4},{4,1},{3,6},{6,3},{9,12},{12,9},{11,14},{14,11},{17,20},{20,... | collective-permute-start | bytes 294920 | tf_op jit(solution)/shard_map/head_grads/ppermute | solution.py:36
  504.1 10.1 %collective-permute-start.18 = (bf16[64,2304]{1,0:T(8,128)(2,1)S(1)}, bf16[64,2304]{1,0:T(8,128)(2,1)S(1)}, u32[]{:S(2)}, u32[]{:S(2)}) collective-permute-start(bf16[64,2304]{1,0:T(8,128)(2,1)S(1)} %broadcast_select_fusion.4), channel_id=1, source_target_pairs={{0,4},{4,0},{1,5},{5,1},{2,6},{6,2},{3,7},{7,3},{8,12},{12,8},{9,1... | collective-permute-start | bytes 884744 | tf_op jit(solution)/shard_map/ffn_grads/ppermute | solution.py:32
  (36 other events, 167.7 us)
Sparse Core Ops, SparseCore 0:
  21.3 122.6 all-gather.1
  270.8 83.1 reduce-scatter.3
